TPU v7x, 512 devices: a whole 4x8x8 slice. The times are simulated.
512 devices in a mesh: bunch: 32 (over y, x), tile: 16 (over z, core).
Axes of the slice: x: 4, y: 8, z: 8, core: 2. Of those that a mesh axis runs over, the one named last changes fastest.
Arguments:
- cell_index: int32 [2, 32, 2, 16384], P(None, 'bunch', None, 'tile'), may hold values from 0 to 255
- charges: bfloat16 [2, 32, 16384], P(None, 'bunch', 'tile'), may hold values from 0.5 to 2
- momenta: float32 [2, 32, 2, 16384], P(None, 'bunch', None, 'tile'), may hold values from -6 to 6
- fill_pattern: int32 [2, 32], P(None, 'bunch'), may hold values 0 or 1
- encounters: int32 [4, 2, 2, 32], P(None, None, None, 'bunch'), may hold values 0 or 1
- green_spectrum: float32 [256, 256], P(None, 'tile'), may hold values from 0.5 to 4
- stop_gain: float32 [4], replicated, may hold values from 0.5 to 2
- parasitic_gain: float32 [4], replicated, may hold values from 0.25 to 1
Outputs:
- kicked: float32 [2, 32, 2, 16384], P(None, 'bunch', None, 'tile')
All inputs are finite; a program needn't handle non-finite values. No bound on the sum of `fill_pattern` or of `encounters` on one device may be relied on, other than what follows from the above.
Results may differ from a plain program's by a relative error of at most 0.0037.
Values may be sent and summed in bfloat16 or wider, within the bound.
A program may use at most 128 MiB of HBM per device.

v0:
```python
import math

import jax
import jax.numpy as jnp
from jax import lax
from jax.sharding import PartitionSpec as P

GRID = 256
STOPS = 4
OFFSET_CELLS = 32


def from_behind(value, axis, steps):
    count = lax.axis_size(axis)
    pairs = [(source, (source + steps) % count) for source in range(count)]
    return lax.ppermute(value, axis, pairs)


def tables(grid):
    positions = jnp.arange(grid, dtype=jnp.int32)
    phases = (positions[:, None] * positions[None, :] % grid).astype(jnp.float32) * (
        2.0 * math.pi / grid
    )
    return (jnp.cos(phases), jnp.sin(phases))


def transform(matrix, operand):
    return jnp.einsum("mi,ibn->mbn", matrix, operand, precision=lax.Precision.HIGHEST)


def shifted_up(operand, amount):
    kept = operand[..., : GRID - amount]
    widths = [(0, 0)] * (operand.ndim - 1) + [(amount, 0)]
    return jnp.pad(kept, widths)


def shifted_down(operand, amount):
    kept = operand[..., amount:]
    widths = [(0, 0)] * (operand.ndim - 1) + [(0, amount)]
    return jnp.pad(kept, widths)


def pick_rows(field_b, rows_p, cols_p):
    row_count = field_b.shape[0]
    inside = (rows_p >= 0) & (rows_p < row_count)
    safe_row = jnp.clip(rows_p, 0, row_count - 1)
    values = field_b[safe_row, :, cols_p].astype(jnp.float32)
    return jnp.where(inside[:, None], values, 0.0).T


def encounter_sum(partners, encounter_marks, stop_gain, parasitic_gain):
    summed = jnp.zeros(partners[0].shape, jnp.float32)
    for stop_number in range(STOPS):
        summed = summed + stop_gain[stop_number] * partners[stop_number].astype(jnp.float32)
        weight = stop_gain[stop_number] * parasitic_gain[stop_number]
        mark_up = encounter_marks[stop_number, 0].astype(jnp.float32)[None, :, None, None]
        following = shifted_up(partners[stop_number + 1].astype(jnp.float32), OFFSET_CELLS)
        summed = summed + weight * mark_up * following
        if stop_number >= 1:
            mark_down = encounter_marks[stop_number, 1].astype(jnp.float32)[None, :, None, None]
            earlier = shifted_down(partners[stop_number - 1].astype(jnp.float32), OFFSET_CELLS)
            summed = summed + weight * mark_down * earlier
    return summed.astype(jnp.bfloat16)


def body(
    cell_index,
    charges,
    momenta,
    fill_pattern,
    encounters,
    green_spectrum,
    stop_gain,
    parasitic_gain,
):
    bunches_here = cell_index.shape[1]
    particles = cell_index.shape[3]
    grid_count = 2 * bunches_here
    tile_count = lax.axis_size("tile")
    tile_rows = GRID // tile_count
    row_of = cell_index[:, :, 0].reshape(grid_count, particles)
    col_of = cell_index[:, :, 1].reshape(grid_count, particles)
    masked = (charges * fill_pattern.astype(jnp.bfloat16)[:, :, None]).reshape(
        grid_count, particles
    )
    columns = jnp.arange(GRID, dtype=jnp.int32)
    block_size = min(1024, particles)
    block_count = particles // block_size
    rows_here = jnp.arange(tile_rows * lax.axis_size("tile"), dtype=jnp.int32)

    def deposit_one_grid(operands):
        rows_p, cols_p, weight_p = operands
        blocks = (
            rows_p.reshape(block_count, block_size),
            cols_p.reshape(block_count, block_size),
            weight_p.reshape(block_count, block_size),
        )

        def add_block(running, block):
            rows_b, cols_b, weight_b = block
            left_hot = jnp.where(
                rows_b[:, None] == rows_here[None, :],
                weight_b[:, None],
                jnp.zeros((), jnp.bfloat16),
            )
            right_hot = (cols_b[:, None] == columns[None, :]).astype(jnp.bfloat16)
            return (
                running
                + jnp.einsum("pr,pc->rc", left_hot, right_hot, preferred_element_type=jnp.float32),
                None,
            )

        start = jnp.zeros((tile_rows * lax.axis_size("tile"), GRID), jnp.float32)
        result, unused = lax.scan(add_block, start, blocks)
        return result

    per_grid = lax.map(deposit_one_grid, (row_of, col_of, masked))
    charge = lax.psum_scatter(
        jnp.transpose(per_grid, (1, 0, 2)), "tile", scatter_dimension=0, tiled=True
    )
    cosine_table, sine_table = tables(GRID)
    real_part = jnp.einsum("rbg,gn->rbn", charge, cosine_table, precision=lax.Precision.HIGHEST)
    imag_part = -jnp.einsum("rbg,gn->rbn", charge, sine_table, precision=lax.Precision.HIGHEST)
    halves = jnp.stack([real_part, imag_part], axis=2)
    first_col = lax.axis_index("tile") * tile_rows
    col_wave = jnp.sin(
        2.0
        * math.pi
        / GRID
        * (first_col + jnp.arange(tile_rows, dtype=jnp.int32)).astype(jnp.float32)
    )
    row_wave = jnp.sin(2.0 * math.pi / GRID * jnp.arange(GRID, dtype=jnp.int32).astype(jnp.float32))
    columns_block = lax.all_to_all(halves, "tile", split_axis=3, concat_axis=0, tiled=True)
    real_in = columns_block[:, :, 0]
    imag_in = columns_block[:, :, 1]
    spec_real = transform(cosine_table, real_in) + transform(sine_table, imag_in)
    spec_imag = transform(cosine_table, imag_in) - transform(sine_table, real_in)
    pot_real = green_spectrum[:, None, :] * spec_real
    pot_imag = green_spectrum[:, None, :] * spec_imag
    outputs = []
    for sine_wave in (row_wave[:, None, None], col_wave[None, None, :]):
        even_part = sine_wave * pot_imag
        odd_part = -sine_wave * pot_real
        outputs.append(transform(cosine_table, even_part) - transform(sine_table, odd_part))
        outputs.append(transform(sine_table, even_part) + transform(cosine_table, odd_part))
    stacked = jnp.stack(outputs, axis=2)
    returned = lax.all_to_all(stacked, "tile", split_axis=0, concat_axis=3, tiled=True)
    inverse_norm = 1.0 / (GRID * GRID)
    field_x = (
        jnp.einsum("rbn,nj->rbj", returned[:, :, 0], cosine_table, precision=lax.Precision.HIGHEST)
        - jnp.einsum("rbn,nj->rbj", returned[:, :, 1], sine_table, precision=lax.Precision.HIGHEST)
    ) * inverse_norm
    field_y = (
        jnp.einsum("rbn,nj->rbj", returned[:, :, 2], cosine_table, precision=lax.Precision.HIGHEST)
        - jnp.einsum("rbn,nj->rbj", returned[:, :, 3], sine_table, precision=lax.Precision.HIGHEST)
    ) * inverse_norm
    fields = jnp.stack([field_x, field_y], axis=2).astype(jnp.bfloat16)
    beam_first = fields[:, :bunches_here]
    beam_second = fields[:, bunches_here:]
    from_above = [beam_second]
    from_below = [beam_first]
    moving_second = beam_second
    moving_first = beam_first
    for offset in range(1, STOPS + 1):
        moving_second = from_behind(moving_second, "bunch", -1)
        moving_first = from_behind(moving_first, "bunch", 1)
        from_above.append(moving_second)
        from_below.append(moving_first)
    total_first = encounter_sum(from_above, encounters[:, 0], stop_gain, parasitic_gain)
    total_second = encounter_sum(from_below, encounters[:, 1], stop_gain, parasitic_gain)
    totals = jnp.concatenate([total_first, total_second], axis=1)

    def add_one_grid(operands):
        field_b, rows_p, cols_p = operands
        return pick_rows(field_b, rows_p, cols_p)

    kick_sum = lax.map(
        add_one_grid,
        (
            jnp.transpose(lax.all_gather(totals, "tile", axis=0, tiled=True), (1, 0, 2, 3)),
            row_of,
            col_of,
        ),
    )
    return momenta + kick_sum.reshape(2, bunches_here, 2, particles)


def solution(mesh):
    in_specs = (
        P(None, "bunch", None, "tile"),
        P(None, "bunch", "tile"),
        P(None, "bunch", None, "tile"),
        P(None, "bunch"),
        P(None, None, None, "bunch"),
        P(None, "tile"),
        P(),
        P(),
    )
    out_specs = P(None, "bunch", None, "tile")
    return jax.shard_map(body, mesh=mesh, in_specs=in_specs, out_specs=out_specs, check_vma=False)
```

profile of v0, /device:TPU:1, one launch (start us, length us, event | category | flops | bytes accessed | tf_op | source)
XLA Modules:
  0.0 271.1 jit_solution(11180594290852846728)
XLA Ops:
  8.8 1.8 while.30
  12.2 62.1 %reduce-scatter.2.cloned.1.call-done = f32[16,2,256]{2,0,1:T(8,128)} async-done(((f32[256,2,256]{2,0,1:T(8,128)}), f32[16,2,256]{2,0,1:T(8,128)}) %reduce-scatter.2.cloned.1.call-update) | async-done | bytes 32784 | tf_op jit(solution)/shard_map/reduce_scatter | solution.py:118
  74.2 2.0 convolution_bitcast_fusion.1
  76.2 2.0 fusion.17
  78.5 1.4 reshape.198
  79.9 7.4 %all-to-all-start = ((f32[16,1,1024]{2,1,0:T(1,128)}), f32[16,1,1024]{2,1,0:T(1,128)S(1)}, u32[]{:S(2)}, u32[]{:S(2)}) async-start(f32[16,1,1024]{2,1,0:T(1,128)} %reshape.198), calls=%async_computation.1 | async-start | bytes 131072 | tf_op jit(solution)/shard_map/all_to_all | solution.py:133
  87.4 7.7 %all-to-all-done = f32[16,1,1024]{2,1,0:T(1,128)S(1)} async-done(((f32[16,1,1024]{2,1,0:T(1,128)}), f32[16,1,1024]{2,1,0:T(1,128)S(1)}, u32[]{:S(2)}, u32[]{:S(2)}) %all-to-all-start) | async-done | bytes 65568 | tf_op jit(solution)/shard_map/all_to_all | solution.py:133
  104.4 1.3 fusion.59
  105.7 1.3 fusion.61
  108.3 1.5 fusion.42
  109.9 1.3 fusion.55
  114.7 2.1 reshape.200
  116.8 3.5 %all-to-all-start.1 = ((f32[16,1,2048]{2,1,0:T(1,128)}), f32[16,1,2048]{2,1,0:T(1,128)S(1)}, u32[]{:S(2)}, u32[]{:S(2)}) async-start(f32[16,1,2048]{2,1,0:T(1,128)} %reshape.200), calls=%async_computation.2 | async-start | bytes 262144 | tf_op jit(solution)/shard_map/all_to_all | solution.py:147
  122.2 7.2 %all-to-all-done.1 = f32[16,1,2048]{2,1,0:T(1,128)S(1)} async-done(((f32[16,1,2048]{2,1,0:T(1,128)}), f32[16,1,2048]{2,1,0:T(1,128)S(1)}, u32[]{:S(2)}, u32[]{:S(2)}) %all-to-all-start.1) | async-done | bytes 131104 | tf_op jit(solution)/shard_map/all_to_all | solution.py:147
  130.4 1.4 reshape.201
  137.8 6.6 %collective-permute-start = (bf16[16,1,2,256]{3,0,1,2:T(8,128)(2,1)S(1)}, bf16[16,1,2,256]{3,0,1,2:T(8,128)(2,1)S(1)}, u32[]{:S(2)}, u32[]{:S(2)}) collective-permute-start(bf16[16,1,2,256]{3,0,1,2:T(8,128)(2,1)S(1)} %get-tuple-element.186), channel_id=1, source_target_pairs={{0,496},{16,0},{32,16},{48,32},{64,48},{80,64},{96,80},{112,96},{1... | collective-permute-start | bytes 49160 | tf_op jit(solution)/shard_map/ppermute | solution.py:16
  158.6 1.9 collective-permute-start.4
  160.6 6.7 %collective-permute-start.1 = (bf16[16,1,2,256]{3,0,1,2:T(8,128)(2,1)S(1)}, bf16[16,1,2,256]{3,0,1,2:T(8,128)(2,1)S(1)}, u32[]{:S(2)}, u32[]{:S(2)}) collective-permute-start(bf16[16,1,2,256]{3,0,1,2:T(8,128)(2,1)S(1)} %collective-permute-done), channel_id=1, source_target_pairs={{0,496},{16,0},{32,16},{48,32},{64,48},{80,64},{96,80},{112,96},{1... | collective-permute-start | bytes 49160 | tf_op jit(solution)/shard_map/ppermute | solution.py:16
  167.4 1.9 collective-permute-start.5
  169.4 6.7 %collective-permute-start.2 = (bf16[16,1,2,256]{3,0,1,2:T(8,128)(2,1)S(1)}, bf16[16,1,2,256]{3,0,1,2:T(8,128)(2,1)S(1)}, u32[]{:S(2)}, u32[]{:S(2)}) collective-permute-start(bf16[16,1,2,256]{3,0,1,2:T(8,128)(2,1)S(1)} %collective-permute-done.1), channel_id=1, source_target_pairs={{0,496},{16,0},{32,16},{48,32},{64,48},{80,64},{96,80},{112,96},{1... | collective-permute-start | bytes 49160 | tf_op jit(solution)/shard_map/ppermute | solution.py:16
  176.1 1.9 collective-permute-start.6
  178.0 6.7 %collective-permute-start.3 = (bf16[16,1,2,256]{3,0,1,2:T(8,128)(2,1)S(1)}, bf16[16,1,2,256]{3,0,1,2:T(8,128)(2,1)S(1)}, u32[]{:S(2)}, u32[]{:S(2)}) collective-permute-start(bf16[16,1,2,256]{3,0,1,2:T(8,128)(2,1)S(1)} %collective-permute-done.2), channel_id=1, source_target_pairs={{0,496},{16,0},{32,16},{48,32},{64,48},{80,64},{96,80},{112,96},{1... | collective-permute-start | bytes 49160 | tf_op jit(solution)/shard_map/ppermute | solution.py:16
  184.8 1.9 collective-permute-start.7
  186.8 2.5 add_convert_fusion.1
  189.2 3.4 %collective-permute-done.7 = bf16[16,1,2,256]{3,0,1,2:T(8,128)(2,1)S(1)} collective-permute-done((bf16[16,1,2,256]{3,0,1,2:T(8,128)(2,1)S(1)}, bf16[16,1,2,256]{3,0,1,2:T(8,128)(2,1)S(1)}, u32[]{:S(2)}, u32[]{:S(2)}) %collective-permute-start.7) | collective-permute-done | bytes 16416 | tf_op jit(solution)/shard_map/ppermute | solution.py:16
  192.6 2.5 add_convert_fusion
  195.1 18.9 %all_gather.3 = bf16[256,2,2,256]{3,0,1,2:T(8,128)(2,1)S(1)} all-gather(bf16[16,2,2,256]{3,0,1,2:T(8,128)(2,1)S(1)} %pad_maximum_fusion.2), channel_id=1, replica_groups=mesh['bunch'=32,'tile'=16] {'tile'}, dimensions={0}, use_global_device_ids=true | all-gather | bytes 557056 | tf_op jit(solution)/shard_map/all_gather | solution.py:180
  214.0 49.6 %while.29 = (s32[]{:T(128)}, f32[2,2,1024]{2,1,0:T(2,128)S(1)}, s32[2,1024]{1,0:T(2,128)S(1)}, bf16[2,256,2,256]{3,1,0,2:T(8,128)(2,1)S(1)}, s32[2,1024]{1,0:T(2,128)S(1)}, /*index=5*/s32[]{:T(128)}) while((s32[]{:T(128)}, f32[2,2,1024]{2,1,0:T(2,128)S(1)}, s32[2,1024]{1,0:T(2,128)S(1)}, bf16[2,256,2,256]{3,1,0,2:T(8,128)(2,1)S(1)}, ...), condition=%wide.region_4.5_spmd, body=%wide.region_3.4_spmd.sunk | while | flops 19458 | bytes 1128533 | solution.py:177
  214.1 11.9 %copy.94 = bf16[1,256,2,256]{2,3,1,0:T(8,128)(2,1)} copy(bf16[1,256,2,256]{3,1,0,2:T(8,128)(2,1)S(1)} %constant_dynamic-slice_fusion.5) | data formatting | bytes 524288 | tf_op jit(solution)/shard_map/while/body/jit(dynamic_index_in_dim)/dynamic_slice | solution.py:177
  226.0 12.4 %gather_fusion = bf16[1024,2]{1,0:T(8,128)(2,1)S(1)} fusion(bf16[256,2,256]{1,2,0:T(8,128)(2,1)} %bitcast.203, s32[1024]{0:T(1024)S(1)} %bitcast.202), kind=kCustom, calls=%fused_computation.clone.1 | custom fusion | bytes 16384 | tf_op jit(solution)/shard_map/while/body/eval_jaxpr/gather | solution.py:47
  239.0 11.9 %copy.94 = bf16[1,256,2,256]{2,3,1,0:T(8,128)(2,1)} copy(bf16[1,256,2,256]{3,1,0,2:T(8,128)(2,1)S(1)} %constant_dynamic-slice_fusion.5) | data formatting | bytes 524288 | tf_op jit(solution)/shard_map/while/body/jit(dynamic_index_in_dim)/dynamic_slice | solution.py:177
  250.9 12.3 %gather_fusion = bf16[1024,2]{1,0:T(8,128)(2,1)S(1)} fusion(bf16[256,2,256]{1,2,0:T(8,128)(2,1)} %bitcast.203, s32[1024]{0:T(1024)S(1)} %bitcast.202), kind=kCustom, calls=%fused_computation.clone.1 | custom fusion | bytes 16384 | tf_op jit(solution)/shard_map/while/body/eval_jaxpr/gather | solution.py:47
  (91 shorter events, 31.5 us)
Async XLA Ops:
  6.5 96.4 %copy-start.1 = (f32[256,16]{0,1:T(8,128)S(1)}, f32[256,16]{0,1:T(8,128)}, u32[]{:S(2)}) copy-start(f32[256,16]{0,1:T(8,128)} %param.17) | copy-start | bytes 49156
  6.5 113.7 %copy-start.3 = (f32[4]{0:T(128)S(1)}, f32[4]{0:T(128)}, u32[]{:S(2)}) copy-start(f32[4]{0:T(128)} %param.18) | copy-start | bytes 52
  6.5 67.7 %reduce-scatter.2.cloned.1.call-start = ((), (), s32[]{:S(2)}) async-start(), calls=%async_computation.3 | async-start | bytes 557056 | tf_op jit(solution)/shard_map/reduce_scatter | solution.py:118
  10.6 0.8 copy-start
  10.6 133.7 %copy-start.4 = (f32[4]{0:T(128)S(1)}, f32[4]{0:T(128)}, u32[]{:S(2)}) copy-start(f32[4]{0:T(128)} %param.19) | copy-start | bytes 52
  79.9 15.2 %all-to-all-start = ((f32[16,1,1024]{2,1,0:T(1,128)}), f32[16,1,1024]{2,1,0:T(1,128)S(1)}, u32[]{:S(2)}, u32[]{:S(2)}) async-start(f32[16,1,1024]{2,1,0:T(1,128)} %reshape.198), calls=%async_computation.1 | async-start | bytes 131072 | tf_op jit(solution)/shard_map/all_to_all | solution.py:133
  116.8 12.7 %all-to-all-start.1 = ((f32[16,1,2048]{2,1,0:T(1,128)}), f32[16,1,2048]{2,1,0:T(1,128)S(1)}, u32[]{:S(2)}, u32[]{:S(2)}) async-start(f32[16,1,2048]{2,1,0:T(1,128)} %reshape.200), calls=%async_computation.2 | async-start | bytes 262144 | tf_op jit(solution)/shard_map/all_to_all | solution.py:147
  137.8 22.8 %collective-permute-start = (bf16[16,1,2,256]{3,0,1,2:T(8,128)(2,1)S(1)}, bf16[16,1,2,256]{3,0,1,2:T(8,128)(2,1)S(1)}, u32[]{:S(2)}, u32[]{:S(2)}) collective-permute-start(bf16[16,1,2,256]{3,0,1,2:T(8,128)(2,1)S(1)} %get-tuple-element.186), channel_id=1, source_target_pairs={{0,496},{16,0},{32,16},{48,32},{64,48},{80,64},{96,80},{112,96},{1... | collective-permute-start | bytes 49160 | tf_op jit(solution)/shard_map/ppermute | solution.py:16
  158.6 8.8 %collective-permute-start.4 = (bf16[16,1,2,256]{3,0,1,2:T(8,128)(2,1)S(1)}, bf16[16,1,2,256]{3,0,1,2:T(8,128)(2,1)S(1)}, u32[]{:S(2)}, u32[]{:S(2)}) collective-permute-start(bf16[16,1,2,256]{3,0,1,2:T(8,128)(2,1)S(1)} %get-tuple-element.187), channel_id=1, source_target_pairs={{0,16},{16,32},{32,48},{48,64},{64,80},{80,96},{96,112},{112,128},... | collective-permute-start | bytes 49160 | tf_op jit(solution)/shard_map/ppermute | solution.py:16
  160.6 8.8 %collective-permute-start.1 = (bf16[16,1,2,256]{3,0,1,2:T(8,128)(2,1)S(1)}, bf16[16,1,2,256]{3,0,1,2:T(8,128)(2,1)S(1)}, u32[]{:S(2)}, u32[]{:S(2)}) collective-permute-start(bf16[16,1,2,256]{3,0,1,2:T(8,128)(2,1)S(1)} %collective-permute-done), channel_id=1, source_target_pairs={{0,496},{16,0},{32,16},{48,32},{64,48},{80,64},{96,80},{112,96},{1... | collective-permute-start | bytes 49160 | tf_op jit(solution)/shard_map/ppermute | solution.py:16
  167.4 8.8 %collective-permute-start.5 = (bf16[16,1,2,256]{3,0,1,2:T(8,128)(2,1)S(1)}, bf16[16,1,2,256]{3,0,1,2:T(8,128)(2,1)S(1)}, u32[]{:S(2)}, u32[]{:S(2)}) collective-permute-start(bf16[16,1,2,256]{3,0,1,2:T(8,128)(2,1)S(1)} %collective-permute-done.4), channel_id=1, source_target_pairs={{0,16},{16,32},{32,48},{48,64},{64,80},{80,96},{96,112},{112,128},... | collective-permute-start | bytes 49160 | tf_op jit(solution)/shard_map/ppermute | solution.py:16
  169.4 8.7 %collective-permute-start.2 = (bf16[16,1,2,256]{3,0,1,2:T(8,128)(2,1)S(1)}, bf16[16,1,2,256]{3,0,1,2:T(8,128)(2,1)S(1)}, u32[]{:S(2)}, u32[]{:S(2)}) collective-permute-start(bf16[16,1,2,256]{3,0,1,2:T(8,128)(2,1)S(1)} %collective-permute-done.1), channel_id=1, source_target_pairs={{0,496},{16,0},{32,16},{48,32},{64,48},{80,64},{96,80},{112,96},{1... | collective-permute-start | bytes 49160 | tf_op jit(solution)/shard_map/ppermute | solution.py:16
  176.1 8.7 %collective-permute-start.6 = (bf16[16,1,2,256]{3,0,1,2:T(8,128)(2,1)S(1)}, bf16[16,1,2,256]{3,0,1,2:T(8,128)(2,1)S(1)}, u32[]{:S(2)}, u32[]{:S(2)}) collective-permute-start(bf16[16,1,2,256]{3,0,1,2:T(8,128)(2,1)S(1)} %collective-permute-done.5), channel_id=1, source_target_pairs={{0,16},{16,32},{32,48},{48,64},{64,80},{80,96},{96,112},{112,128},... | collective-permute-start | bytes 49160 | tf_op jit(solution)/shard_map/ppermute | solution.py:16
  178.0 8.7 %collective-permute-start.3 = (bf16[16,1,2,256]{3,0,1,2:T(8,128)(2,1)S(1)}, bf16[16,1,2,256]{3,0,1,2:T(8,128)(2,1)S(1)}, u32[]{:S(2)}, u32[]{:S(2)}) collective-permute-start(bf16[16,1,2,256]{3,0,1,2:T(8,128)(2,1)S(1)} %collective-permute-done.2), channel_id=1, source_target_pairs={{0,496},{16,0},{32,16},{48,32},{64,48},{80,64},{96,80},{112,96},{1... | collective-permute-start | bytes 49160 | tf_op jit(solution)/shard_map/ppermute | solution.py:16
  184.8 7.8 %collective-permute-start.7 = (bf16[16,1,2,256]{3,0,1,2:T(8,128)(2,1)S(1)}, bf16[16,1,2,256]{3,0,1,2:T(8,128)(2,1)S(1)}, u32[]{:S(2)}, u32[]{:S(2)}) collective-permute-start(bf16[16,1,2,256]{3,0,1,2:T(8,128)(2,1)S(1)} %collective-permute-done.6), channel_id=1, source_target_pairs={{0,16},{16,32},{32,48},{48,64},{64,80},{80,96},{96,112},{112,128},... | collective-permute-start | bytes 49160 | tf_op jit(solution)/shard_map/ppermute | solution.py:16
  214.0 49.6 %copy-start.2 = (f32[2,1,2,1024]{3,2,1,0:T(2,128)S(1)}, f32[2,1,2,1024]{3,2,1,0:T(2,128)}, u32[]{:S(2)}) copy-start(f32[2,1,2,1024]{3,2,1,0:T(2,128)} %param.14) | copy-start | bytes 49156
Sparse Core Ops, SparseCore 0:
  11.6 62.6 reduce-scatter.1
where the time goes:
time: 272 us; the launch traced here: 271 us
  waiting for transfers between devices  80.5 us (30%)
  local copies, waits for them, and re-layouts  63.2 us (23%)
  starting transfers between devices  45.1 us (17%)
  between operations  27.4 us (10%)
  matrix products  26.5 us (10%)
  blocking collectives  18.9 us (7%)
  other arithmetic  9.5 us (3%)
    reduce_scatter x1, waiting for transfers between devices, body(): lax.psum_scatter(jnp.transpose(per_grid, (1, 0, 2)), 'tile', scatter_dime...  62.1 us
    ppermute x8, starting transfers between devices, from_behind(): return lax.ppermute(value, axis, pairs)  34.3 us
    gather x2, local copies, waits for them, and re-layouts, pick_rows(): values = field_b[safe_row, :, cols_p].astype(jnp.float32)  24.7 us
    dynamic_slice x4, local copies, waits for them, and re-layouts, body(): lax.map(add_one_grid, (jnp.transpose(lax.all_gather(totals, 'tile', axis=...  23.9 us
    all_gather x1, blocking collectives, body(): lax.all_gather(totals, 'tile', axis=0, tiled=True)  18.9 us
    unnamed x12, matrix products  16 us
    all_to_all x1, waiting for transfers between devices, body(): lax.all_to_all(halves, 'tile', split_axis=3, concat_axis=0, tiled=True)  7.72 us
    all_to_all x1, starting transfers between devices, body(): lax.all_to_all(halves, 'tile', split_axis=3, concat_axis=0, tiled=True)  7.36 us
  transfers between devices with their start and end apart: 11, of which 4 were waited for; matrix products, arithmetic and copies ran while one was open for 2% of the time, Pallas kernels for 0%

commit v1 on v0

v1 whole, which is shorter than its diff:
```python
import functools
import math

import jax
import jax.numpy as jnp
import ml_dtypes
import numpy as np
from jax import lax
from jax.experimental import pallas as pl
from jax.experimental.pallas import tpu as pltpu
from jax.sharding import PartitionSpec as P

GRID = 256
HALF = GRID // 2
STOPS = 4
OFFSET_CELLS = 32
CHIPS = 8
SLAB = GRID // CHIPS
PAIR = SLAB // 2
CHUNK = 256
MESH = pl.DeviceIdType.MESH
F32 = jnp.float32
BF16 = jnp.bfloat16
RING_ORDER = (4, 3, 5, 2, 6, 1, 7)


def split_np(table):
    high = table.astype(ml_dtypes.bfloat16)
    low = (table - high.astype(np.float64)).astype(ml_dtypes.bfloat16)
    return high, low


def basis_rows(wave, is_sine):
    positions = np.arange(GRID)
    if is_sine and wave == 0:
        return np.cos(math.pi * positions) / 16.0
    if wave == 0:
        return np.full(GRID, 1.0 / 16.0)
    angle = 2.0 * math.pi / GRID * ((wave * positions) % GRID)
    return (np.sin(angle) if is_sine else np.cos(angle)) * math.sqrt(2.0) / 16.0


def fold_row(wave, is_sine):
    row = np.zeros(GRID)
    if wave == 0:
        row[HALF if is_sine else 0] = 1.0
    else:
        row[wave] = 0.5
        row[GRID - wave] = -0.5 if is_sine else 0.5
    return row


def make_tables():
    slab_order = [
        (PAIR * chip + r % PAIR, r >= PAIR) for chip in range(CHIPS) for r in range(SLAB)
    ]
    plain_order = [(q % HALF, q >= HALF) for q in range(GRID)]
    row_basis = np.stack([basis_rows(*entry) for entry in slab_order])
    col_basis = np.stack([basis_rows(*entry) for entry in plain_order])
    row_fold = np.stack([fold_row(*entry) for entry in slab_order])
    col_fold = np.stack([fold_row(*entry) for entry in plain_order]).T
    stacked = np.stack(
        [
            *split_np(row_basis),
            *split_np(col_basis.T),
            *split_np(col_basis),
            row_fold.astype(ml_dtypes.bfloat16),
            col_fold.astype(ml_dtypes.bfloat16),
        ]
    )
    sines = np.sin(2.0 * math.pi / GRID * np.arange(HALF))
    return stacked, np.repeat(sines[:, None], 128, axis=1).astype(np.float32)


def split(value):
    high = value.astype(BF16)
    return high, (value - high.astype(F32)).astype(BF16)


def mm(a, b):
    return jnp.dot(a, b, preferred_element_type=F32)


def mm_nt(a, b):
    return lax.dot_general(a, b, (((1,), (1,)), ((), ())), preferred_element_type=F32)


def mm3(a, b):
    return mm(a[0], b[0]) + (mm(a[0], b[1]) + mm(a[1], b[0]))


def kernel(
    bunches,
    cell_ref,
    charge_ref,
    momenta_ref,
    fill_ref,
    mark_ref,
    green_ref,
    stop_ref,
    para_ref,
    table_ref,
    sine_ref,
    out_ref,
    cells,
    charge,
    charge_other,
    momenta,
    fill,
    marks,
    green,
    stop,
    para,
    table,
    sines,
    wide,
    pack_mine,
    pack_other,
    pack_out,
    pack_in,
    row_hot,
    col_hot,
    row_wave,
    row_wave_low,
    rows_out,
    rows_in,
    spec_out,
    spec_in,
    total,
    kick_out,
    kick_in,
    load_sem,
    swap_send,
    swap_recv,
    pack_send,
    pack_recv,
    rows_send,
    rows_recv,
    spec_send,
    spec_recv,
    total_send,
    total_recv,
    kick_send,
    kick_recv,
):
    parts = cells.shape[2]
    bunch = lax.axis_index("bunch")
    tile = lax.axis_index("tile")
    chip = lax.div(tile, 2)
    core = lax.rem(tile, 2)
    other = 1 - core
    sibling = (bunch, 2 * chip + other)

    def ring(step):
        there = lax.rem(chip + step, CHIPS)
        return there, (bunch, 2 * there + core)

    def meets(step):
        return (lax.rem(bunch + (1 - 2 * core) * step + 4 * bunches, bunches), 2 * chip + other)

    barrier = pltpu.get_barrier_semaphore()
    partners = [meets(step) for step in range(STOPS + 1)] + [ring(step)[1] for step in range(1, CHIPS)]
    for partner in partners:
        pl.semaphore_signal(barrier, inc=1, device_id=partner, device_id_type=MESH)

    loads = [
        pltpu.make_async_copy(source, target, load_sem.at[index])
        for index, (source, target) in enumerate(
            [
                (green_ref, green),
                (table_ref, table),
                (cell_ref.at[core, 0], cells.at[0]),
                (charge_ref, charge),
                (fill_ref, fill),
                (mark_ref, marks),
                (stop_ref, stop),
                (para_ref, para),
                (sine_ref, sines),
                (momenta_ref, momenta),
            ]
        )
    ]
    for load in loads:
        load.start()

    row_basis = (table.at[0], table.at[1])
    to_cols = (table.at[2], table.at[3])
    from_cols = (table.at[4], table.at[5])

    loads[0].wait()
    loads[1].wait()
    wide[...] = jnp.zeros(wide.shape, F32)
    wide[0 : green.shape[0]] = green[...]
    green_high, green_low = split(wide[...])
    folded = mm_nt(table[6], green_high) + mm_nt(table[6], green_low)
    folded = folded.reshape(CHIPS, 4, 8, 128)
    packed = folded[:, 0].reshape(CHIPS * 8, 128)
    for group in range(1, 4):
        packed = packed + pltpu.roll(folded[:, group].reshape(CHIPS * 8, 128), 32 * group, 1)
    packed = pltpu.roll(packed, 16 * core, 1)
    pack_mine[...] = packed.reshape(CHIPS, 8, 128)

    pl.semaphore_wait(barrier, len(partners))

    swaps = [
        pltpu.make_async_remote_copy(
            src_ref=source,
            dst_ref=target,
            send_sem=swap_send.at[index],
            recv_sem=swap_recv.at[index],
            device_id=sibling,
            device_id_type=MESH,
        )
        for index, (source, target) in enumerate(
            [
                (cell_ref.at[other, 0], cells.at[1]),
                (charge_ref, charge_other),
                (pack_mine, pack_other),
            ]
        )
    ]
    for swap in swaps:
        swap.start()

    cell_iota = lax.broadcasted_iota(jnp.int32, (GRID, CHUNK), 0)

    def deposit(half):
        filled = fill[core].astype(F32)
        for first in range(0, parts, CHUNK):
            here = pl.ds(half * parts + first, CHUNK)
            rows = cells[half, 0:1, first : first + CHUNK]
            cols = cells[half, 1:2, first : first + CHUNK]
            both = (charge, charge_other)[half][:, first : first + CHUNK].astype(F32)
            weight = jnp.where(core == 0, both[0:1], both[1:2]) * filled
            row_hot[:, here] = jnp.where(cell_iota == rows, 1.0, 0.0).astype(BF16)
            col_hot[:, here] = jnp.where(cell_iota == cols, weight, 0.0).astype(BF16)
        span = pl.ds(half * parts, parts)
        return mm_nt(row_hot[:, span], col_hot[:, span])

    for load in loads[2:]:
        load.wait()
    density = deposit(0)
    for swap in swaps:
        swap.wait()

    pack_out[...] = pack_mine[...] + pack_other[...]
    pack_in[chip] = pack_out[chip]
    packs = []
    for step in RING_ORDER:
        there, device = ring(step)
        copy = pltpu.make_async_remote_copy(
            src_ref=pack_out.at[there],
            dst_ref=pack_in.at[chip],
            send_sem=pack_send.at[step],
            recv_sem=pack_recv.at[step],
            device_id=device,
            device_id_type=MESH,
        )
        copy.start()
        packs.append(copy)

    density = density + deposit(1)
    basis_high, basis_low = row_basis[0][...], row_basis[1][...]
    partial = mm3((basis_high, basis_low), split(density))
    rows_out[...] = partial.astype(BF16)
    top = partial[0:16]
    first_row = lax.broadcasted_iota(jnp.int32, top.shape, 0) == 0
    rows_out[0:16, :] = jnp.where(first_row, top - jnp.mean(top, axis=1, keepdims=True), top).astype(BF16)
    sums = []
    for step in RING_ORDER:
        there, device = ring(step)
        copy = pltpu.make_async_remote_copy(
            src_ref=rows_out.at[pl.ds(pl.multiple_of(SLAB * there, SLAB), SLAB)],
            dst_ref=rows_in.at[step],
            send_sem=rows_send.at[step],
            recv_sem=rows_recv.at[step],
            device_id=device,
            device_id_type=MESH,
        )
        copy.start()
        sums.append(copy)

    row_wave[...] = mm(basis_high, row_hot[...]).astype(BF16)
    row_wave_low[...] = mm(basis_low, row_hot[...]).astype(BF16)

    for copy in packs:
        copy.wait()
    lane = lax.broadcasted_iota(jnp.int32, (8, 128), 1)
    halves = []
    for side in range(2):
        groups = []
        for group in range(4):
            merged = jnp.zeros((8, 128), F32)
            for spot in range(4):
                moved = pack_in[4 * side + spot]
                shift = (32 * (spot - group)) % 128
                if shift:
                    moved = pltpu.roll(moved, shift, 1)
                merged = jnp.where(lane // 32 == spot, moved, merged)
            groups.append(merged)
        halves.append(jnp.concatenate(groups, axis=0))
    slab_high, slab_low = split(jnp.concatenate(halves, axis=1))
    factors = mm(slab_high, table[7]) + mm(slab_low, table[7])
    lanes = lax.broadcasted_iota(jnp.int32, (PAIR, HALF), 1)
    subs = lax.broadcasted_iota(jnp.int32, (PAIR, HALF), 0)
    special = jnp.logical_and(subs == 0, chip == 0)
    gain_cc = factors[:PAIR, :HALF]
    gain_cs = jnp.where(lanes == 0, factors[:PAIR, HALF:], gain_cc)
    gain_sc = jnp.where(special, factors[PAIR:, :HALF], gain_cc)
    gain_ss = jnp.where(special, jnp.where(lanes == 0, factors[PAIR:, HALF:], factors[PAIR:, :HALF]), gain_cs)
    mixing = jnp.where(jnp.logical_or(special, lanes == 0), 0.0, factors[PAIR:, HALF:])

    for copy in sums:
        copy.wait()
    slab = rows_out[pl.ds(pl.multiple_of(SLAB * chip, SLAB), SLAB), :].astype(F32)
    for step in range(1, CHIPS):
        slab = slab + rows_in[step].astype(F32)
    spectrum = mm3(split(slab), (to_cols[0][...], to_cols[1][...]))
    part_cc, part_cs = spectrum[:PAIR, :HALF], spectrum[:PAIR, HALF:]
    part_sc, part_ss = spectrum[PAIR:, :HALF], spectrum[PAIR:, HALF:]
    upper = jnp.concatenate(
        [gain_cc * part_cc - mixing * part_ss, gain_cs * part_cs + mixing * part_sc], axis=1
    )
    lower = jnp.concatenate(
        [gain_sc * part_sc + mixing * part_cs, gain_ss * part_ss - mixing * part_cc], axis=1
    )
    spec_out[...] = jnp.concatenate([upper, lower], axis=0).astype(spec_out.dtype)
    spectra = []
    for step in (3, 2, 4, 1, 0):
        copy = pltpu.make_async_remote_copy(
            src_ref=spec_out,
            dst_ref=spec_in.at[step],
            send_sem=spec_send.at[step],
            recv_sem=spec_recv.at[step],
            device_id=meets(step),
            device_id_type=MESH,
        )
        copy.start()
        spectra.append(copy)

    gains = [stop[s] for s in range(STOPS)]
    weights = [stop[s] * para[s] for s in range(STOPS)]
    marks_up = [marks[2 * core, s].astype(F32) for s in range(STOPS)]
    marks_down = [marks[2 * core + 1, s].astype(F32) for s in range(STOPS)]
    for copy in spectra:
        copy.wait()
    direct = jnp.zeros((SLAB, GRID), F32)
    upward = jnp.zeros((SLAB, GRID), F32)
    downward = jnp.zeros((SLAB, GRID), F32)
    for step in range(STOPS + 1):
        partner = spec_in[step].astype(F32)
        if step < STOPS:
            direct = direct + gains[step] * partner
        if step >= 1:
            upward = upward + (weights[step - 1] * marks_up[step - 1]) * partner
        if step + 1 < STOPS:
            downward = downward + (weights[step + 1] * marks_down[step + 1]) * partner
    mixed = mm3(
        split(jnp.concatenate([direct, upward, downward], axis=0)),
        (from_cols[0][...], from_cols[1][...]),
    )
    column = lax.broadcasted_iota(jnp.int32, (SLAB, GRID), 1)

    def encounter(three):
        moved_up = jnp.where(column >= OFFSET_CELLS, pltpu.roll(three[SLAB : 2 * SLAB], OFFSET_CELLS, 1), 0.0)
        moved_down = jnp.where(
            column < GRID - OFFSET_CELLS, pltpu.roll(three[2 * SLAB :], GRID - OFFSET_CELLS, 1), 0.0
        )
        return three[:SLAB] + moved_up + moved_down

    smooth = encounter(mixed)
    sine = sines[pl.ds(pl.multiple_of(PAIR * chip, PAIR), PAIR), :]
    sine = jnp.concatenate([sine, sine], axis=1)
    along_x = jnp.concatenate([-sine * smooth[PAIR:], sine * smooth[:PAIR]], axis=0)
    along_y = encounter(-0.5 * (pltpu.roll(mixed, GRID - 1, 1) - pltpu.roll(mixed, 1, 1)))
    mine = pl.ds(pl.multiple_of(SLAB * chip, SLAB), SLAB)
    total[mine, :] = jnp.concatenate([along_x, along_y], axis=1).astype(BF16)
    gathers = []
    for step in RING_ORDER:
        there, device = ring(step)
        copy = pltpu.make_async_remote_copy(
            src_ref=total.at[mine],
            dst_ref=total.at[mine],
            send_sem=total_send.at[step],
            recv_sem=total_recv.at[step],
            device_id=device,
            device_id_type=MESH,
        )
        copy.start()
        gathers.append(copy)
    for copy in gathers:
        copy.wait()

    turned = jnp.transpose(total[...].astype(F32)).astype(BF16)

    def kicks(half, target):
        for first in range(0, parts, CHUNK):
            here = pl.ds(half * parts + first, CHUNK)
            values = mm(turned, row_wave[:, here]) + mm(turned, row_wave_low[:, here])
            hit = cell_iota == cells[half, 1:2, first : first + CHUNK]
            for axis in range(2):
                picked = jnp.where(hit, values[axis * GRID : (axis + 1) * GRID], 0.0)
                target(axis, first, jnp.sum(picked, axis=0, keepdims=True))

    def to_sibling(axis, first, value):
        kick_out[axis : axis + 1, first : first + CHUNK] = value

    def to_output(axis, first, value):
        out_ref[core, 0, axis : axis + 1, first : first + CHUNK] = (
            momenta[core, 0, axis : axis + 1, first : first + CHUNK] + value
        )

    kicks(1, to_sibling)
    back = pltpu.make_async_remote_copy(
        src_ref=kick_out,
        dst_ref=kick_in,
        send_sem=kick_send,
        recv_sem=kick_recv,
        device_id=sibling,
        device_id_type=MESH,
    )
    back.start()
    kicks(0, to_output)
    back.wait()
    out_ref[other, 0] = momenta[other, 0] + kick_in[...]


def body(bunches, tables, *operands):
    cell_index, charges, momenta, fill_pattern, encounters, green_spectrum, stop_gain, parasitic_gain = operands
    parts = cell_index.shape[3]
    stacked, sines = tables
    charges = charges.reshape(2, parts)
    fill_pattern = fill_pattern.reshape(2)
    encounters = encounters.reshape(STOPS, 2, 2).transpose(1, 2, 0).reshape(4, STOPS)
    green_spectrum = green_spectrum.T
    operands = (cell_index, charges, momenta, fill_pattern, encounters, green_spectrum, stop_gain, parasitic_gain)
    any_spec = pl.BlockSpec(memory_space=pltpu.HBM)
    dma = pltpu.SemaphoreType.DMA
    return pl.pallas_call(
        functools.partial(kernel, bunches),
        out_shape=jax.ShapeDtypeStruct(momenta.shape, F32),
        in_specs=[any_spec] * 10,
        out_specs=pl.BlockSpec(memory_space=pltpu.VMEM),
        scratch_shapes=[
            pltpu.VMEM((2, 2, parts), jnp.int32),
            pltpu.VMEM((2, parts), BF16),
            pltpu.VMEM((2, parts), BF16),
            pltpu.VMEM((2, 1, 2, parts), F32),
            pltpu.SMEM(fill_pattern.shape, jnp.int32),
            pltpu.SMEM(encounters.shape, jnp.int32),
            pltpu.VMEM(green_spectrum.shape, F32),
            pltpu.SMEM(stop_gain.shape, F32),
            pltpu.SMEM(parasitic_gain.shape, F32),
            pltpu.VMEM(stacked.shape, BF16),
            pltpu.VMEM(sines.shape, F32),
            pltpu.VMEM((128, GRID), F32),
            pltpu.VMEM((CHIPS, 8, 128), F32),
            pltpu.VMEM((CHIPS, 8, 128), F32),
            pltpu.VMEM((CHIPS, 8, 128), F32),
            pltpu.VMEM((CHIPS, 8, 128), F32),
            pltpu.VMEM((GRID, 2 * parts), BF16),
            pltpu.VMEM((GRID, 2 * parts), BF16),
            pltpu.VMEM((GRID, 2 * parts), BF16),
            pltpu.VMEM((GRID, 2 * parts), BF16),
            pltpu.VMEM((GRID, GRID), BF16),
            pltpu.VMEM((CHIPS, SLAB, GRID), BF16),
            pltpu.VMEM((SLAB, GRID), F32),
            pltpu.VMEM((STOPS + 1, SLAB, GRID), F32),
            pltpu.VMEM((GRID, 2 * GRID), BF16),
            pltpu.VMEM((2, parts), F32),
            pltpu.VMEM((2, parts), F32),
            dma((10,)),
            dma((3,)),
            dma((3,)),
            dma((CHIPS,)),
            dma((CHIPS,)),
            dma((CHIPS,)),
            dma((CHIPS,)),
            dma((STOPS + 1,)),
            dma((STOPS + 1,)),
            dma((CHIPS,)),
            dma((CHIPS,)),
            dma(()),
            dma(()),
        ],
        compiler_params=pltpu.CompilerParams(
            collective_id=0, has_side_effects=True, vmem_limit_bytes=60 << 20
        ),
    )(*operands, stacked, sines)


def solution(mesh):
    in_specs = (
        P(None, "bunch", None, "tile"),
        P(None, "bunch", "tile"),
        P(None, "bunch", None, "tile"),
        P(None, "bunch"),
        P(None, None, None, "bunch"),
        P(None, "tile"),
        P(),
        P(),
    )
    out_specs = P(None, "bunch", None, "tile")
    tables = make_tables()
    return jax.shard_map(
        functools.partial(body, mesh.shape["bunch"], tables),
        mesh=mesh,
        in_specs=in_specs,
        out_specs=out_specs,
        check_vma=False,
    )
```

time: 272 us -> 39.1 us (0.14)
  waiting for transfers between devices: 80.5 us -> 0 us
  local copies, waits for them, and re-layouts: 63.2 us -> 1.32 us
  starting transfers between devices: 45.1 us -> 0 us
  Pallas kernels: 0 us -> 37.5 us
  between operations: 27.4 us -> 0.01 us
  matrix products: 26.5 us -> 0 us
  blocking collectives: 18.9 us -> 0 us
  other arithmetic: 9.5 us -> 0 us
    reduce_scatter x1 -> x0, waiting for transfers between devices: 62.1 us -> none  [body(): lax.psum_scatter(jnp.transpose(per_grid, (1, 0, 2)), 'tile', scatter_dime...]
    pallas_call x0 -> x1, Pallas kernels: none -> 37.5 us  [body(): pl.pallas_call(functools.partial(kernel, bunches), out_shape=jax.ShapeDty...]
    ppermute x8 -> x0, starting transfers between devices: 34.3 us -> none  [from_behind(): return lax.ppermute(value, axis, pairs)]
    gather x2 -> x0, local copies, waits for them, and re-layouts: 24.7 us -> none  [pick_rows(): values = field_b[safe_row, :, cols_p].astype(jnp.float32)]
    dynamic_slice x8 -> x0, local copies, waits for them, and re-layouts: 23.9 us -> none  [the longest x4 23.9 us: body(): lax.map(add_one_grid, (jnp.transpose(lax.all_gather(totals, 'tile', axis=...]
    all_gather x1 -> x0, blocking collectives: 18.9 us -> none  [body(): lax.all_gather(totals, 'tile', axis=0, tiled=True)]
    unnamed x12 -> x0, matrix products: 16 us -> none
    all_to_all x2 -> x0, waiting for transfers between devices: 14.9 us -> none  [the longest x1 7.72 us: body(): lax.all_to_all(halves, 'tile', split_axis=3, concat_axis=0, tiled=True)]
  transfers between devices with their start and end apart: 11 -> 0, of which waited for: 4 -> 0; matrix products, arithmetic and copies ran while one was open for 2% -> 0% of each run, Pallas kernels for 0% -> 0%
where the time goes in v1:
time: 39.1 us; the launch traced here: 38.8 us
  Pallas kernels  37.5 us (96%)
  local copies, waits for them, and re-layouts  1.32 us (3%)
    pallas_call x1, Pallas kernels, body(): pl.pallas_call(functools.partial(kernel, bunches), out_shape=jax.ShapeDty...  37.5 us
    unnamed x1, local copies, waits for them, and re-layouts  1.32 us

profile of v1, /device:TPU:1, one launch (start us, length us, event | category | flops | bytes accessed | tf_op | source)
XLA Modules:
  0.0 38.8 jit_solution(633164736182410067)
XLA Ops:
  0.0 37.5 %shard_map.100 = f32[2,1,2,1024]{3,2,1,0:T(2,128)} custom-call(s32[2,1,2,1024]{3,2,1,0:T(2,128)} %cell_ref.1, bf16[2,1024]{1,0:T(2,128)(2,1)} %bitcast.9, f32[2,1,2,1024]{3,2,1,0:T(2,128)} %momenta_ref.1, s32[2]{0:T(128)} %bitcast.11, s32[4,4]{1,0:T(4,128)} %bitcast.10, f32[16,256]{1,0:T(8,128)} %bitcast.8, f32[4]{0:T(128)} %stop_ref.1, f32[4]{0:T(128)} %para_ref.1, ...), custom_call_target="tpu_custom_call" | custom-call | tf_op jit(solution)/shard_map/pallas_call | solution.py:439
  37.5 1.3 %copy.12 = f32[2,1,2,1024]{3,2,1,0:T(2,128)} copy(f32[2,1,2,1024]{3,2,1,0:T(2,128)} %shard_map.100) | data formatting | bytes 32768

commit v2 on v1

--- a/solution.py
+++ b/solution.py
@@ -16,8 +16,11 @@
 OFFSET_CELLS = 32
 CHIPS = 8
 SLAB = GRID // CHIPS
-PAIR = SLAB // 2
+HALVES = 2
+PART = SLAB // HALVES
+PAIR = PART // 2
 CHUNK = 256
+LEAD = 4
 MESH = pl.DeviceIdType.MESH
 F32 = jnp.float32
 BF16 = jnp.bfloat16
@@ -52,7 +55,7 @@
 
 def make_tables():
     slab_order = [
-        (PAIR * chip + r % PAIR, r >= PAIR) for chip in range(CHIPS) for r in range(SLAB)
+        (PAIR * part + r % PAIR, r >= PAIR) for part in range(CHIPS * HALVES) for r in range(PART)
     ]
     plain_order = [(q % HALF, q >= HALF) for q in range(GRID)]
     row_basis = np.stack([basis_rows(*entry) for entry in slab_order])
@@ -142,6 +145,8 @@
     total_recv,
     kick_send,
     kick_recv,
+    ring_in,
+    met_in,
 ):
     parts = cells.shape[2]
     bunch = lax.axis_index("bunch")
@@ -159,9 +164,15 @@
         return (lax.rem(bunch + (1 - 2 * core) * step + 4 * bunches, bunches), 2 * chip + other)
 
     barrier = pltpu.get_barrier_semaphore()
-    partners = [meets(step) for step in range(STOPS + 1)] + [ring(step)[1] for step in range(1, CHIPS)]
-    for partner in partners:
+    leads = lax.rem(chip, LEAD) == 0
+    near = [sibling] + [ring(step)[1] for step in range(1, CHIPS)]
+    for partner in near:
         pl.semaphore_signal(barrier, inc=1, device_id=partner, device_id_type=MESH)
+
+    @pl.when(leads)
+    def _():
+        for step in range(1, STOPS + 1):
+            pl.semaphore_signal(barrier, inc=1, device_id=meets(step), device_id_type=MESH)
 
     loads = [
         pltpu.make_async_copy(source, target, load_sem.at[index])
@@ -200,7 +211,12 @@
     packed = pltpu.roll(packed, 16 * core, 1)
     pack_mine[...] = packed.reshape(CHIPS, 8, 128)
 
-    pl.semaphore_wait(barrier, len(partners))
+    pl.semaphore_wait(barrier, jnp.where(leads, len(near) + STOPS, len(near)))
+
+    @pl.when(leads)
+    def _():
+        for step in range(1, STOPS + 1):
+            pl.semaphore_signal(ring_in, inc=1, device_id=meets(step), device_id_type=MESH)
 
     swaps = [
         pltpu.make_async_remote_copy(
@@ -266,22 +282,31 @@
     top = partial[0:16]
     first_row = lax.broadcasted_iota(jnp.int32, top.shape, 0) == 0
     rows_out[0:16, :] = jnp.where(first_row, top - jnp.mean(top, axis=1, keepdims=True), top).astype(BF16)
-    sums = []
-    for step in RING_ORDER:
-        there, device = ring(step)
-        copy = pltpu.make_async_remote_copy(
-            src_ref=rows_out.at[pl.ds(pl.multiple_of(SLAB * there, SLAB), SLAB)],
-            dst_ref=rows_in.at[step],
-            send_sem=rows_send.at[step],
-            recv_sem=rows_recv.at[step],
-            device_id=device,
-            device_id_type=MESH,
-        )
-        copy.start()
-        sums.append(copy)
+    sums = [[] for _ in range(HALVES)]
+    for part in range(HALVES):
+        for step in RING_ORDER:
+            there, device = ring(step)
+            first = pl.multiple_of(SLAB * there + PART * part, PART)
+            copy = pltpu.make_async_remote_copy(
+                src_ref=rows_out.at[pl.ds(first, PART)],
+                dst_ref=rows_in.at[part, step],
+                send_sem=rows_send.at[part, step],
+                recv_sem=rows_recv.at[part, step],
+                device_id=device,
+                device_id_type=MESH,
+            )
+            copy.start()
+            sums[part].append(copy)
 
     row_wave[...] = mm(basis_high, row_hot[...]).astype(BF16)
     row_wave_low[...] = mm(basis_low, row_hot[...]).astype(BF16)
+
+    @pl.when(leads)
+    def _():
+        pl.semaphore_wait(ring_in, STOPS)
+        for ahead in range(1, LEAD):
+            follower = (bunch, 2 * (chip + ahead) + core)
+            pl.semaphore_signal(met_in, inc=1, device_id=follower, device_id_type=MESH)
 
     for copy in packs:
         copy.wait()
@@ -303,91 +328,107 @@
     factors = mm(slab_high, table[7]) + mm(slab_low, table[7])
     lanes = lax.broadcasted_iota(jnp.int32, (PAIR, HALF), 1)
     subs = lax.broadcasted_iota(jnp.int32, (PAIR, HALF), 0)
-    special = jnp.logical_and(subs == 0, chip == 0)
-    gain_cc = factors[:PAIR, :HALF]
-    gain_cs = jnp.where(lanes == 0, factors[:PAIR, HALF:], gain_cc)
-    gain_sc = jnp.where(special, factors[PAIR:, :HALF], gain_cc)
-    gain_ss = jnp.where(special, jnp.where(lanes == 0, factors[PAIR:, HALF:], factors[PAIR:, :HALF]), gain_cs)
-    mixing = jnp.where(jnp.logical_or(special, lanes == 0), 0.0, factors[PAIR:, HALF:])
-
-    for copy in sums:
-        copy.wait()
-    slab = rows_out[pl.ds(pl.multiple_of(SLAB * chip, SLAB), SLAB), :].astype(F32)
-    for step in range(1, CHIPS):
-        slab = slab + rows_in[step].astype(F32)
-    spectrum = mm3(split(slab), (to_cols[0][...], to_cols[1][...]))
-    part_cc, part_cs = spectrum[:PAIR, :HALF], spectrum[:PAIR, HALF:]
-    part_sc, part_ss = spectrum[PAIR:, :HALF], spectrum[PAIR:, HALF:]
-    upper = jnp.concatenate(
-        [gain_cc * part_cc - mixing * part_ss, gain_cs * part_cs + mixing * part_sc], axis=1
-    )
-    lower = jnp.concatenate(
-        [gain_sc * part_sc + mixing * part_cs, gain_ss * part_ss - mixing * part_cc], axis=1
-    )
-    spec_out[...] = jnp.concatenate([upper, lower], axis=0).astype(spec_out.dtype)
-    spectra = []
-    for step in (3, 2, 4, 1, 0):
-        copy = pltpu.make_async_remote_copy(
-            src_ref=spec_out,
-            dst_ref=spec_in.at[step],
-            send_sem=spec_send.at[step],
-            recv_sem=spec_recv.at[step],
-            device_id=meets(step),
-            device_id_type=MESH,
-        )
-        copy.start()
-        spectra.append(copy)
+
+    def convolve(part):
+        even = factors[PART * part : PART * part + PAIR]
+        odd = factors[PART * part + PAIR : PART * (part + 1)]
+        gain_cc = even[:, :HALF]
+        gain_cs = jnp.where(lanes == 0, even[:, HALF:], gain_cc)
+        gain_sc, gain_ss, edge = gain_cc, gain_cs, lanes == 0
+        if part == 0:
+            special = jnp.logical_and(subs == 0, chip == 0)
+            gain_sc = jnp.where(special, odd[:, :HALF], gain_cc)
+            gain_ss = jnp.where(special, jnp.where(lanes == 0, odd[:, HALF:], odd[:, :HALF]), gain_cs)
+            edge = jnp.logical_or(special, lanes == 0)
+        mixing = jnp.where(edge, 0.0, odd[:, HALF:])
+        slab = rows_out[pl.ds(pl.multiple_of(SLAB * chip + PART * part, PART), PART), :].astype(F32)
+        for step in range(1, CHIPS):
+            slab = slab + rows_in[part, step].astype(F32)
+        spectrum = mm3(split(slab), (to_cols[0][...], to_cols[1][...]))
+        part_cc, part_cs = spectrum[:PAIR, :HALF], spectrum[:PAIR, HALF:]
+        part_sc, part_ss = spectrum[PAIR:, :HALF], spectrum[PAIR:, HALF:]
+        spec_out[part, :PAIR, :HALF] = gain_cc * part_cc - mixing * part_ss
+        spec_out[part, :PAIR, HALF:] = gain_cs * part_cs + mixing * part_sc
+        spec_out[part, PAIR:, :HALF] = gain_sc * part_sc + mixing * part_cs
+        spec_out[part, PAIR:, HALF:] = gain_ss * part_ss - mixing * part_cc
+
+    spectra = [[] for _ in range(HALVES)]
+    for part in range(HALVES):
+        for copy in sums[part]:
+            copy.wait()
+        convolve(part)
+        if part == 0:
+
+            @pl.when(jnp.logical_not(leads))
+            def _():
+                pl.semaphore_wait(met_in, 1)
+
+        for step in (3, 2, 4, 1, 0):
+            copy = pltpu.make_async_remote_copy(
+                src_ref=spec_out.at[part],
+                dst_ref=spec_in.at[part, step],
+                send_sem=spec_send.at[part, step],
+                recv_sem=spec_recv.at[part, step],
+                device_id=meets(step),
+                device_id_type=MESH,
+            )
+            copy.start()
+            spectra[part].append(copy)
 
     gains = [stop[s] for s in range(STOPS)]
     weights = [stop[s] * para[s] for s in range(STOPS)]
     marks_up = [marks[2 * core, s].astype(F32) for s in range(STOPS)]
     marks_down = [marks[2 * core + 1, s].astype(F32) for s in range(STOPS)]
-    for copy in spectra:
-        copy.wait()
-    direct = jnp.zeros((SLAB, GRID), F32)
-    upward = jnp.zeros((SLAB, GRID), F32)
-    downward = jnp.zeros((SLAB, GRID), F32)
-    for step in range(STOPS + 1):
-        partner = spec_in[step].astype(F32)
-        if step < STOPS:
-            direct = direct + gains[step] * partner
-        if step >= 1:
-            upward = upward + (weights[step - 1] * marks_up[step - 1]) * partner
-        if step + 1 < STOPS:
-            downward = downward + (weights[step + 1] * marks_down[step + 1]) * partner
-    mixed = mm3(
-        split(jnp.concatenate([direct, upward, downward], axis=0)),
-        (from_cols[0][...], from_cols[1][...]),
-    )
-    column = lax.broadcasted_iota(jnp.int32, (SLAB, GRID), 1)
+    column = lax.broadcasted_iota(jnp.int32, (PART, GRID), 1)
 
     def encounter(three):
-        moved_up = jnp.where(column >= OFFSET_CELLS, pltpu.roll(three[SLAB : 2 * SLAB], OFFSET_CELLS, 1), 0.0)
+        moved_up = jnp.where(column >= OFFSET_CELLS, pltpu.roll(three[PART : 2 * PART], OFFSET_CELLS, 1), 0.0)
         moved_down = jnp.where(
-            column < GRID - OFFSET_CELLS, pltpu.roll(three[2 * SLAB :], GRID - OFFSET_CELLS, 1), 0.0
-        )
-        return three[:SLAB] + moved_up + moved_down
-
-    smooth = encounter(mixed)
-    sine = sines[pl.ds(pl.multiple_of(PAIR * chip, PAIR), PAIR), :]
-    sine = jnp.concatenate([sine, sine], axis=1)
-    along_x = jnp.concatenate([-sine * smooth[PAIR:], sine * smooth[:PAIR]], axis=0)
-    along_y = encounter(-0.5 * (pltpu.roll(mixed, GRID - 1, 1) - pltpu.roll(mixed, 1, 1)))
-    mine = pl.ds(pl.multiple_of(SLAB * chip, SLAB), SLAB)
-    total[mine, :] = jnp.concatenate([along_x, along_y], axis=1).astype(BF16)
+            column < GRID - OFFSET_CELLS, pltpu.roll(three[2 * PART :], GRID - OFFSET_CELLS, 1), 0.0
+        )
+        return three[:PART] + moved_up + moved_down
+
+    def collect(part):
+        direct = jnp.zeros((PART, GRID), F32)
+        upward = jnp.zeros((PART, GRID), F32)
+        downward = jnp.zeros((PART, GRID), F32)
+        for step in range(STOPS + 1):
+            partner = spec_in[part, step]
+            if step < STOPS:
+                direct = direct + gains[step] * partner
+            if step >= 1:
+                upward = upward + (weights[step - 1] * marks_up[step - 1]) * partner
+            if step + 1 < STOPS:
+                downward = downward + (weights[step + 1] * marks_down[step + 1]) * partner
+        mixed = mm3(
+            split(jnp.concatenate([direct, upward, downward], axis=0)),
+            (from_cols[0][...], from_cols[1][...]),
+        )
+        smooth = encounter(mixed)
+        sine = sines[pl.ds(pl.multiple_of(PAIR * (HALVES * chip + part), PAIR), PAIR), :]
+        sine = jnp.concatenate([sine, sine], axis=1)
+        along_x = jnp.concatenate([-sine * smooth[PAIR:], sine * smooth[:PAIR]], axis=0)
+        along_y = encounter(-0.5 * (pltpu.roll(mixed, GRID - 1, 1) - pltpu.roll(mixed, 1, 1)))
+        return jnp.concatenate([along_x, along_y], axis=1).astype(BF16)
+
     gathers = []
-    for step in RING_ORDER:
-        there, device = ring(step)
-        copy = pltpu.make_async_remote_copy(
-            src_ref=total.at[mine],
-            dst_ref=total.at[mine],
-            send_sem=total_send.at[step],
-            recv_sem=total_recv.at[step],
-            device_id=device,
-            device_id_type=MESH,
-        )
-        copy.start()
-        gathers.append(copy)
+    for part in range(HALVES):
+        for copy in spectra[part]:
+            copy.wait()
+        mine = pl.ds(pl.multiple_of(SLAB * chip + PART * part, PART), PART)
+        total[mine, :] = collect(part)
+        for step in RING_ORDER:
+            there, device = ring(step)
+            copy = pltpu.make_async_remote_copy(
+                src_ref=total.at[mine],
+                dst_ref=total.at[mine],
+                send_sem=total_send.at[part, step],
+                recv_sem=total_recv.at[part, step],
+                device_id=device,
+                device_id_type=MESH,
+            )
+            copy.start()
+            gathers.append(copy)
     for copy in gathers:
         copy.wait()
 
@@ -463,9 +504,9 @@
             pltpu.VMEM((GRID, 2 * parts), BF16),
             pltpu.VMEM((GRID, 2 * parts), BF16),
             pltpu.VMEM((GRID, GRID), BF16),
-            pltpu.VMEM((CHIPS, SLAB, GRID), BF16),
-            pltpu.VMEM((SLAB, GRID), F32),
-            pltpu.VMEM((STOPS + 1, SLAB, GRID), F32),
+            pltpu.VMEM((HALVES, CHIPS, PART, GRID), BF16),
+            pltpu.VMEM((HALVES, PART, GRID), F32),
+            pltpu.VMEM((HALVES, STOPS + 1, PART, GRID), F32),
             pltpu.VMEM((GRID, 2 * GRID), BF16),
             pltpu.VMEM((2, parts), F32),
             pltpu.VMEM((2, parts), F32),
@@ -474,14 +515,16 @@
             dma((3,)),
             dma((CHIPS,)),
             dma((CHIPS,)),
-            dma((CHIPS,)),
-            dma((CHIPS,)),
-            dma((STOPS + 1,)),
-            dma((STOPS + 1,)),
-            dma((CHIPS,)),
-            dma((CHIPS,)),
+            dma((HALVES, CHIPS)),
+            dma((HALVES, CHIPS)),
+            dma((HALVES, STOPS + 1)),
+            dma((HALVES, STOPS + 1)),
+            dma((HALVES, CHIPS)),
+            dma((HALVES, CHIPS)),
             dma(()),
             dma(()),
+            pltpu.SemaphoreType.REGULAR,
+            pltpu.SemaphoreType.REGULAR,
         ],
         compiler_params=pltpu.CompilerParams(
             collective_id=0, has_side_effects=True, vmem_limit_bytes=60 << 20

time: 39.1 us -> 37.8 us (0.967)
  Pallas kernels: 37.5 us -> 36.2 us
    pallas_call x1, Pallas kernels: 37.5 us -> 36.2 us  [body(): pl.pallas_call(functools.partial(kernel, bunches), out_shape=jax.ShapeDty...]
where the time goes in v2:
time: 37.8 us; the launch traced here: 37.6 us
  Pallas kernels  36.2 us (96%)
  local copies, waits for them, and re-layouts  1.32 us (3%)
    pallas_call x1, Pallas kernels, body(): pl.pallas_call(functools.partial(kernel, bunches), out_shape=jax.ShapeDty...  36.2 us
    unnamed x1, local copies, waits for them, and re-layouts  1.32 us

profile of v2, /device:TPU:1, one launch (start us, length us, event | category | flops | bytes accessed | tf_op | source)
XLA Modules:
  0.0 37.6 jit_solution(493213598210351377)
XLA Ops:
  0.0 36.2 %shard_map.100 = f32[2,1,2,1024]{3,2,1,0:T(2,128)} custom-call(s32[2,1,2,1024]{3,2,1,0:T(2,128)} %cell_ref.1, bf16[2,1024]{1,0:T(2,128)(2,1)} %bitcast.9, f32[2,1,2,1024]{3,2,1,0:T(2,128)} %momenta_ref.1, s32[2]{0:T(128)} %bitcast.11, s32[4,4]{1,0:T(4,128)} %bitcast.10, f32[16,256]{1,0:T(8,128)} %bitcast.8, f32[4]{0:T(128)} %stop_ref.1, f32[4]{0:T(128)} %para_ref.1, ...), custom_call_target="tpu_custom_call" | custom-call | tf_op jit(solution)/shard_map/pallas_call | solution.py:480
  36.2 1.3 %copy.12 = f32[2,1,2,1024]{3,2,1,0:T(2,128)} copy(f32[2,1,2,1024]{3,2,1,0:T(2,128)} %shard_map.100) | data formatting | bytes 32768

commit v3 on v2

--- a/solution.py
+++ b/solution.py
@@ -57,8 +57,14 @@
     slab_order = [
         (PAIR * part + r % PAIR, r >= PAIR) for part in range(CHIPS * HALVES) for r in range(PART)
     ]
+    half_order = [
+        slab_order[SLAB * chip + PART * part + r]
+        for part in range(HALVES)
+        for chip in range(CHIPS)
+        for r in range(PART)
+    ]
     plain_order = [(q % HALF, q >= HALF) for q in range(GRID)]
-    row_basis = np.stack([basis_rows(*entry) for entry in slab_order])
+    row_basis = np.stack([basis_rows(*entry) for entry in half_order])
     col_basis = np.stack([basis_rows(*entry) for entry in plain_order])
     row_fold = np.stack([fold_row(*entry) for entry in slab_order])
     col_fold = np.stack([fold_row(*entry) for entry in plain_order]).T
@@ -124,7 +130,7 @@
     row_hot,
     col_hot,
     row_wave,
-    row_wave_low,
+    kick_first,
     rows_out,
     rows_in,
     spec_out,
@@ -257,7 +263,7 @@
         load.wait()
     density = deposit(0)
     for swap in swaps:
-        swap.wait()
+        swap.wait_recv()
 
     pack_out[...] = pack_mine[...] + pack_other[...]
     pack_in[chip] = pack_out[chip]
@@ -277,16 +283,19 @@
 
     density = density + deposit(1)
     basis_high, basis_low = row_basis[0][...], row_basis[1][...]
-    partial = mm3((basis_high, basis_low), split(density))
-    rows_out[...] = partial.astype(BF16)
+    pieces = split(density)
+    partial = mm3((basis_high[:HALF], basis_low[:HALF]), pieces)
+    rows_out[:HALF, :] = partial.astype(BF16)
     top = partial[0:16]
     first_row = lax.broadcasted_iota(jnp.int32, top.shape, 0) == 0
     rows_out[0:16, :] = jnp.where(first_row, top - jnp.mean(top, axis=1, keepdims=True), top).astype(BF16)
     sums = [[] for _ in range(HALVES)]
     for part in range(HALVES):
+        if part == 1:
+            rows_out[HALF:, :] = mm3((basis_high[HALF:], basis_low[HALF:]), pieces).astype(BF16)
         for step in RING_ORDER:
             there, device = ring(step)
-            first = pl.multiple_of(SLAB * there + PART * part, PART)
+            first = pl.multiple_of(HALF * part + PART * there, PART)
             copy = pltpu.make_async_remote_copy(
                 src_ref=rows_out.at[pl.ds(first, PART)],
                 dst_ref=rows_in.at[part, step],
@@ -298,8 +307,10 @@
             copy.start()
             sums[part].append(copy)
 
-    row_wave[...] = mm(basis_high, row_hot[...]).astype(BF16)
-    row_wave_low[...] = mm(basis_low, row_hot[...]).astype(BF16)
+    for part in range(HALVES):
+        span = slice(HALF * part, HALF * (part + 1))
+        both = jnp.concatenate([basis_high[span], basis_low[span]], axis=0)
+        row_wave[part] = mm(both, row_hot[...]).astype(BF16)
 
     @pl.when(leads)
     def _():
@@ -309,7 +320,7 @@
             pl.semaphore_signal(met_in, inc=1, device_id=follower, device_id_type=MESH)
 
     for copy in packs:
-        copy.wait()
+        copy.wait_recv()
     lane = lax.broadcasted_iota(jnp.int32, (8, 128), 1)
     halves = []
     for side in range(2):
@@ -341,7 +352,7 @@
             gain_ss = jnp.where(special, jnp.where(lanes == 0, odd[:, HALF:], odd[:, :HALF]), gain_cs)
             edge = jnp.logical_or(special, lanes == 0)
         mixing = jnp.where(edge, 0.0, odd[:, HALF:])
-        slab = rows_out[pl.ds(pl.multiple_of(SLAB * chip + PART * part, PART), PART), :].astype(F32)
+        slab = rows_out[pl.ds(pl.multiple_of(HALF * part + PART * chip, PART), PART), :].astype(F32)
         for step in range(1, CHIPS):
             slab = slab + rows_in[part, step].astype(F32)
         spectrum = mm3(split(slab), (to_cols[0][...], to_cols[1][...]))
@@ -355,7 +366,7 @@
     spectra = [[] for _ in range(HALVES)]
     for part in range(HALVES):
         for copy in sums[part]:
-            copy.wait()
+            copy.wait_recv()
         convolve(part)
         if part == 0:
 
@@ -363,7 +374,7 @@
             def _():
                 pl.semaphore_wait(met_in, 1)
 
-        for step in (3, 2, 4, 1, 0):
+        for step in (4, 3, 2, 1, 0):
             copy = pltpu.make_async_remote_copy(
                 src_ref=spec_out.at[part],
                 dst_ref=spec_in.at[part, step],
@@ -411,11 +422,11 @@
         along_y = encounter(-0.5 * (pltpu.roll(mixed, GRID - 1, 1) - pltpu.roll(mixed, 1, 1)))
         return jnp.concatenate([along_x, along_y], axis=1).astype(BF16)
 
-    gathers = []
+    gathers = [[] for _ in range(HALVES)]
     for part in range(HALVES):
         for copy in spectra[part]:
-            copy.wait()
-        mine = pl.ds(pl.multiple_of(SLAB * chip + PART * part, PART), PART)
+            copy.wait_recv()
+        mine = pl.ds(pl.multiple_of(HALF * part + PART * chip, PART), PART)
         total[mine, :] = collect(part)
         for step in RING_ORDER:
             there, device = ring(step)
@@ -428,30 +439,39 @@
                 device_id_type=MESH,
             )
             copy.start()
-            gathers.append(copy)
-    for copy in gathers:
-        copy.wait()
-
-    turned = jnp.transpose(total[...].astype(F32)).astype(BF16)
-
-    def kicks(half, target):
+            gathers[part].append(copy)
+    def kicks(part, half, turned, target):
         for first in range(0, parts, CHUNK):
-            here = pl.ds(half * parts + first, CHUNK)
-            values = mm(turned, row_wave[:, here]) + mm(turned, row_wave_low[:, here])
+            values = mm(turned, row_wave[part, :, pl.ds(half * parts + first, CHUNK)])
             hit = cell_iota == cells[half, 1:2, first : first + CHUNK]
             for axis in range(2):
                 picked = jnp.where(hit, values[axis * GRID : (axis + 1) * GRID], 0.0)
-                target(axis, first, jnp.sum(picked, axis=0, keepdims=True))
-
-    def to_sibling(axis, first, value):
-        kick_out[axis : axis + 1, first : first + CHUNK] = value
-
-    def to_output(axis, first, value):
+                target(half, axis, first, jnp.sum(picked, axis=0, keepdims=True))
+
+    def turn(part):
+        for copy in gathers[part]:
+            copy.wait_recv()
+        rows = jnp.transpose(total[HALF * part : HALF * (part + 1), :].astype(F32)).astype(BF16)
+        return jnp.concatenate([rows, rows], axis=1)
+
+    def keep(half, axis, first, value):
+        kick_first[half, axis : axis + 1, first : first + CHUNK] = value
+
+    def to_sibling(half, axis, first, value):
+        before = kick_first[half, axis : axis + 1, first : first + CHUNK]
+        kick_out[axis : axis + 1, first : first + CHUNK] = before + value
+
+    def to_output(half, axis, first, value):
+        before = kick_first[half, axis : axis + 1, first : first + CHUNK]
         out_ref[core, 0, axis : axis + 1, first : first + CHUNK] = (
-            momenta[core, 0, axis : axis + 1, first : first + CHUNK] + value
-        )
-
-    kicks(1, to_sibling)
+            momenta[core, 0, axis : axis + 1, first : first + CHUNK] + (before + value)
+        )
+
+    turned = turn(0)
+    kicks(0, 1, turned, keep)
+    kicks(0, 0, turned, keep)
+    turned = turn(1)
+    kicks(1, 1, turned, to_sibling)
     back = pltpu.make_async_remote_copy(
         src_ref=kick_out,
         dst_ref=kick_in,
@@ -461,9 +481,11 @@
         device_id_type=MESH,
     )
     back.start()
-    kicks(0, to_output)
-    back.wait()
+    kicks(1, 0, turned, to_output)
+    back.wait_recv()
     out_ref[other, 0] = momenta[other, 0] + kick_in[...]
+    for copy in [*swaps, *packs, *sums[0], *sums[1], *spectra[0], *spectra[1], *gathers[0], *gathers[1], back]:
+        copy.wait_send()
 
 
 def body(bunches, tables, *operands):
@@ -501,8 +523,8 @@
             pltpu.VMEM((CHIPS, 8, 128), F32),
             pltpu.VMEM((GRID, 2 * parts), BF16),
             pltpu.VMEM((GRID, 2 * parts), BF16),
-            pltpu.VMEM((GRID, 2 * parts), BF16),
-            pltpu.VMEM((GRID, 2 * parts), BF16),
+            pltpu.VMEM((HALVES, GRID, 2 * parts), BF16),
+            pltpu.VMEM((2, 2, parts), F32),
             pltpu.VMEM((GRID, GRID), BF16),
             pltpu.VMEM((HALVES, CHIPS, PART, GRID), BF16),
             pltpu.VMEM((HALVES, PART, GRID), F32),

time: 37.8 us -> 36.8 us (0.974)
  Pallas kernels: 36.2 us -> 35.1 us
    pallas_call x1, Pallas kernels: 36.2 us -> 35.1 us  [body(): pl.pallas_call(functools.partial(kernel, bunches), out_shape=jax.ShapeDty...]
where the time goes in v3:
time: 36.8 us; the launch traced here: 36.5 us
  Pallas kernels  35.1 us (95%)
  local copies, waits for them, and re-layouts  1.32 us (4%)
    pallas_call x1, Pallas kernels, body(): pl.pallas_call(functools.partial(kernel, bunches), out_shape=jax.ShapeDty...  35.1 us
    unnamed x1, local copies, waits for them, and re-layouts  1.32 us

profile of v3, /device:TPU:1, one launch (start us, length us, event | category | flops | bytes accessed | tf_op | source)
XLA Modules:
  0.0 36.5 jit_solution(669993877022174674)
XLA Ops:
  0.0 35.1 %shard_map.100 = f32[2,1,2,1024]{3,2,1,0:T(2,128)} custom-call(s32[2,1,2,1024]{3,2,1,0:T(2,128)} %cell_ref.1, bf16[2,1024]{1,0:T(2,128)(2,1)} %bitcast.9, f32[2,1,2,1024]{3,2,1,0:T(2,128)} %momenta_ref.1, s32[2]{0:T(128)} %bitcast.11, s32[4,4]{1,0:T(4,128)} %bitcast.10, f32[16,256]{1,0:T(8,128)} %bitcast.8, f32[4]{0:T(128)} %stop_ref.1, f32[4]{0:T(128)} %para_ref.1, ...), custom_call_target="tpu_custom_call" | custom-call | tf_op jit(solution)/shard_map/pallas_call | solution.py:502
  35.2 1.3 %copy.12 = f32[2,1,2,1024]{3,2,1,0:T(2,128)} copy(f32[2,1,2,1024]{3,2,1,0:T(2,128)} %shard_map.100) | data formatting | bytes 32768

commit v4 on v3

--- a/solution.py
+++ b/solution.py
@@ -102,7 +102,6 @@
     bunches,
     cell_ref,
     charge_ref,
-    momenta_ref,
     fill_ref,
     mark_ref,
     green_ref,
@@ -114,7 +113,6 @@
     cells,
     charge,
     charge_other,
-    momenta,
     fill,
     marks,
     green,
@@ -129,6 +127,7 @@
     pack_in,
     row_hot,
     col_hot,
+    col_plain,
     row_wave,
     kick_first,
     rows_out,
@@ -137,7 +136,7 @@
     spec_in,
     total,
     kick_out,
-    kick_in,
+    kick_own,
     load_sem,
     swap_send,
     swap_recv,
@@ -151,6 +150,7 @@
     total_recv,
     kick_send,
     kick_recv,
+    own_sem,
     ring_in,
     met_in,
 ):
@@ -193,7 +193,6 @@
                 (stop_ref, stop),
                 (para_ref, para),
                 (sine_ref, sines),
-                (momenta_ref, momenta),
             ]
         )
     ]
@@ -307,10 +306,11 @@
             copy.start()
             sums[part].append(copy)
 
-    for part in range(HALVES):
-        span = slice(HALF * part, HALF * (part + 1))
-        both = jnp.concatenate([basis_high[span], basis_low[span]], axis=0)
-        row_wave[part] = mm(both, row_hot[...]).astype(BF16)
+    for first in range(0, 2 * parts, CHUNK):
+        here = pl.ds(first, CHUNK)
+        row_wave[:, here] = mm(basis_high, row_hot[:, here]) + mm(basis_low, row_hot[:, here])
+        cols = cells[first // parts, 1:2, first % parts : first % parts + CHUNK]
+        col_plain[:, here] = jnp.where(cell_iota == cols, 1.0, 0.0).astype(BF16)
 
     @pl.when(leads)
     def _():
@@ -428,31 +428,41 @@
             copy.wait_recv()
         mine = pl.ds(pl.multiple_of(HALF * part + PART * chip, PART), PART)
         total[mine, :] = collect(part)
-        for step in RING_ORDER:
-            there, device = ring(step)
+        for place in range(CHIPS - 1):
+            there = place + jnp.where(place >= chip, 1, 0)
+            step = lax.rem(there - chip + CHIPS, CHIPS)
             copy = pltpu.make_async_remote_copy(
                 src_ref=total.at[mine],
                 dst_ref=total.at[mine],
-                send_sem=total_send.at[part, step],
+                send_sem=total_send.at[part, place],
                 recv_sem=total_recv.at[part, step],
-                device_id=device,
+                device_id=(bunch, 2 * there + core),
                 device_id_type=MESH,
             )
             copy.start()
             gathers[part].append(copy)
-    def kicks(part, half, turned, target):
+    def kicks(part, half, target):
+        span = slice(HALF * part, HALF * (part + 1))
+        stacked = jnp.concatenate([total[span, :GRID], total[span, GRID:]], axis=0)
         for first in range(0, parts, CHUNK):
-            values = mm(turned, row_wave[part, :, pl.ds(half * parts + first, CHUNK)])
-            hit = cell_iota == cells[half, 1:2, first : first + CHUNK]
+            here = pl.ds(half * parts + first, CHUNK)
+            values = mm(stacked, col_plain[:, here])
+            wave = row_wave[span, here]
             for axis in range(2):
-                picked = jnp.where(hit, values[axis * GRID : (axis + 1) * GRID], 0.0)
+                picked = values[axis * HALF : (axis + 1) * HALF] * wave
                 target(half, axis, first, jnp.sum(picked, axis=0, keepdims=True))
 
-    def turn(part):
-        for copy in gathers[part]:
-            copy.wait_recv()
-        rows = jnp.transpose(total[HALF * part : HALF * (part + 1), :].astype(F32)).astype(BF16)
-        return jnp.concatenate([rows, rows], axis=1)
+    def arrive(part):
+        mine = pl.ds(pl.multiple_of(HALF * part + PART * chip, PART), PART)
+        for step in range(1, CHIPS):
+            pltpu.make_async_remote_copy(
+                src_ref=total.at[mine],
+                dst_ref=total.at[mine],
+                send_sem=total_send.at[part, 0],
+                recv_sem=total_recv.at[part, step],
+                device_id=ring(step)[1],
+                device_id_type=MESH,
+            ).wait_recv()
 
     def keep(half, axis, first, value):
         kick_first[half, axis : axis + 1, first : first + CHUNK] = value
@@ -463,27 +473,27 @@
 
     def to_output(half, axis, first, value):
         before = kick_first[half, axis : axis + 1, first : first + CHUNK]
-        out_ref[core, 0, axis : axis + 1, first : first + CHUNK] = (
-            momenta[core, 0, axis : axis + 1, first : first + CHUNK] + (before + value)
-        )
-
-    turned = turn(0)
-    kicks(0, 1, turned, keep)
-    kicks(0, 0, turned, keep)
-    turned = turn(1)
-    kicks(1, 1, turned, to_sibling)
+        kick_own[axis : axis + 1, first : first + CHUNK] = before + value
+
+    arrive(0)
+    kicks(0, 1, keep)
+    kicks(0, 0, keep)
+    arrive(1)
+    kicks(1, 1, to_sibling)
     back = pltpu.make_async_remote_copy(
         src_ref=kick_out,
-        dst_ref=kick_in,
+        dst_ref=out_ref.at[core, 0],
         send_sem=kick_send,
         recv_sem=kick_recv,
         device_id=sibling,
         device_id_type=MESH,
     )
     back.start()
-    kicks(1, 0, turned, to_output)
+    kicks(1, 0, to_output)
+    here = pltpu.make_async_copy(kick_own, out_ref.at[core, 0], own_sem)
+    here.start()
+    here.wait()
     back.wait_recv()
-    out_ref[other, 0] = momenta[other, 0] + kick_in[...]
     for copy in [*swaps, *packs, *sums[0], *sums[1], *spectra[0], *spectra[1], *gathers[0], *gathers[1], back]:
         copy.wait_send()
 
@@ -496,19 +506,18 @@
     fill_pattern = fill_pattern.reshape(2)
     encounters = encounters.reshape(STOPS, 2, 2).transpose(1, 2, 0).reshape(4, STOPS)
     green_spectrum = green_spectrum.T
-    operands = (cell_index, charges, momenta, fill_pattern, encounters, green_spectrum, stop_gain, parasitic_gain)
+    operands = (cell_index, charges, fill_pattern, encounters, green_spectrum, stop_gain, parasitic_gain)
     any_spec = pl.BlockSpec(memory_space=pltpu.HBM)
     dma = pltpu.SemaphoreType.DMA
-    return pl.pallas_call(
+    kicks = pl.pallas_call(
         functools.partial(kernel, bunches),
         out_shape=jax.ShapeDtypeStruct(momenta.shape, F32),
-        in_specs=[any_spec] * 10,
-        out_specs=pl.BlockSpec(memory_space=pltpu.VMEM),
+        in_specs=[any_spec] * 9,
+        out_specs=any_spec,
         scratch_shapes=[
             pltpu.VMEM((2, 2, parts), jnp.int32),
             pltpu.VMEM((2, parts), BF16),
             pltpu.VMEM((2, parts), BF16),
-            pltpu.VMEM((2, 1, 2, parts), F32),
             pltpu.SMEM(fill_pattern.shape, jnp.int32),
             pltpu.SMEM(encounters.shape, jnp.int32),
             pltpu.VMEM(green_spectrum.shape, F32),
@@ -523,7 +532,8 @@
             pltpu.VMEM((CHIPS, 8, 128), F32),
             pltpu.VMEM((GRID, 2 * parts), BF16),
             pltpu.VMEM((GRID, 2 * parts), BF16),
-            pltpu.VMEM((HALVES, GRID, 2 * parts), BF16),
+            pltpu.VMEM((GRID, 2 * parts), BF16),
+            pltpu.VMEM((GRID, 2 * parts), F32),
             pltpu.VMEM((2, 2, parts), F32),
             pltpu.VMEM((GRID, GRID), BF16),
             pltpu.VMEM((HALVES, CHIPS, PART, GRID), BF16),
@@ -532,7 +542,7 @@
             pltpu.VMEM((GRID, 2 * GRID), BF16),
             pltpu.VMEM((2, parts), F32),
             pltpu.VMEM((2, parts), F32),
-            dma((10,)),
+            dma((9,)),
             dma((3,)),
             dma((3,)),
             dma((CHIPS,)),
@@ -545,6 +555,7 @@
             dma((HALVES, CHIPS)),
             dma(()),
             dma(()),
+            dma(()),
             pltpu.SemaphoreType.REGULAR,
             pltpu.SemaphoreType.REGULAR,
         ],
@@ -552,6 +563,7 @@
             collective_id=0, has_side_effects=True, vmem_limit_bytes=60 << 20
         ),
     )(*operands, stacked, sines)
+    return momenta + kicks
 
 
 def solution(mesh):

time: 36.8 us -> 36.5 us (level)
  other arithmetic: 0 us -> 1.33 us
  local copies, waits for them, and re-layouts: 1.32 us -> 0.01 us
    add x0 -> x1, other arithmetic: none -> 1.33 us  [body(): return momenta + kicks]
    unnamed x1 -> x2, local copies, waits for them, and re-layouts: 1.32 us -> 0.01 us
where the time goes in v4:
time: 36.5 us; the launch traced here: 36.2 us
  Pallas kernels  34.9 us (96%)
  other arithmetic  1.33 us (4%)
    pallas_call x1, Pallas kernels, body(): pl.pallas_call(functools.partial(kernel, bunches), out_shape=jax.ShapeDty...  34.9 us
    add x1, other arithmetic, body(): return momenta + kicks  1.33 us

profile of v4, /device:TPU:1, one launch (start us, length us, event | category | flops | bytes accessed | tf_op | source)
XLA Modules:
  0.0 36.2 jit_solution(2471702225200161610)
XLA Ops:
  0.0 0.0 copy-start
  0.0 34.9 %shard_map.100 = f32[2,1,2,1024]{3,2,1,0:T(2,128)} custom-call(s32[2,1,2,1024]{3,2,1,0:T(2,128)} %cell_ref.1, bf16[2,1024]{1,0:T(2,128)(2,1)} %bitcast.9, s32[2]{0:T(128)} %bitcast.11, s32[4,4]{1,0:T(4,128)} %bitcast.10, f32[16,256]{1,0:T(8,128)} %bitcast.8, f32[4]{0:T(128)} %stop_ref.1, f32[4]{0:T(128)} %para_ref.1, ...), custom_call_target="tpu_custom_call" | custom-call | tf_op jit(solution)/shard_map/pallas_call | solution.py:512
  34.9 0.0 copy-done
  34.9 1.3 %add.3 = f32[2,1,2,1024]{3,2,1,0:T(2,128)} add(f32[2,1,2,1024]{3,2,1,0:T(2,128)S(1)} %copy-done, f32[2,1,2,1024]{3,2,1,0:T(2,128)} %shard_map.100) | non-fusion elementwise | flops 4096 | bytes 49152 | tf_op jit(solution)/shard_map/add | solution.py:566
Async XLA Ops:
  0.0 34.9 %copy-start = (f32[2,1,2,1024]{3,2,1,0:T(2,128)S(1)}, f32[2,1,2,1024]{3,2,1,0:T(2,128)}, u32[]{:S(2)}) copy-start(f32[2,1,2,1024]{3,2,1,0:T(2,128)} %param.12) | copy-start | bytes 49156

commit v5 on v4

--- a/solution.py
+++ b/solution.py
@@ -429,8 +429,12 @@
         mine = pl.ds(pl.multiple_of(HALF * part + PART * chip, PART), PART)
         total[mine, :] = collect(part)
         for place in range(CHIPS - 1):
-            there = place + jnp.where(place >= chip, 1, 0)
-            step = lax.rem(there - chip + CHIPS, CHIPS)
+            if part == 0:
+                step = RING_ORDER[place]
+                there = ring(step)[0]
+            else:
+                there = place + jnp.where(place >= chip, 1, 0)
+                step = lax.rem(there - chip + CHIPS, CHIPS)
             copy = pltpu.make_async_remote_copy(
                 src_ref=total.at[mine],
                 dst_ref=total.at[mine],

time: 36.5 us -> 36.4 us (level)
  no operation moved by 1% of the time
where the time goes in v5:
time: 36.4 us; the launch traced here: 36.1 us
  Pallas kernels  34.7 us (95%)
  other arithmetic  1.33 us (4%)
    pallas_call x1, Pallas kernels, body(): pl.pallas_call(functools.partial(kernel, bunches), out_shape=jax.ShapeDty...  34.7 us
    add x1, other arithmetic, body(): return momenta + kicks  1.33 us

profile of v5, /device:TPU:1, one launch (start us, length us, event | category | flops | bytes accessed | tf_op | source)
XLA Modules:
  0.0 36.1 jit_solution(13690632943298619390)
XLA Ops:
  0.0 0.0 copy-start
  0.0 34.7 %shard_map.100 = f32[2,1,2,1024]{3,2,1,0:T(2,128)} custom-call(s32[2,1,2,1024]{3,2,1,0:T(2,128)} %cell_ref.1, bf16[2,1024]{1,0:T(2,128)(2,1)} %bitcast.9, s32[2]{0:T(128)} %bitcast.11, s32[4,4]{1,0:T(4,128)} %bitcast.10, f32[16,256]{1,0:T(8,128)} %bitcast.8, f32[4]{0:T(128)} %stop_ref.1, f32[4]{0:T(128)} %para_ref.1, ...), custom_call_target="tpu_custom_call" | custom-call | tf_op jit(solution)/shard_map/pallas_call | solution.py:516
  34.7 0.0 copy-done
  34.7 1.3 %add.3 = f32[2,1,2,1024]{3,2,1,0:T(2,128)} add(f32[2,1,2,1024]{3,2,1,0:T(2,128)S(1)} %copy-done, f32[2,1,2,1024]{3,2,1,0:T(2,128)} %shard_map.100) | non-fusion elementwise | flops 4096 | bytes 49152 | tf_op jit(solution)/shard_map/add | solution.py:570
Async XLA Ops:
  0.0 34.7 %copy-start = (f32[2,1,2,1024]{3,2,1,0:T(2,128)S(1)}, f32[2,1,2,1024]{3,2,1,0:T(2,128)}, u32[]{:S(2)}) copy-start(f32[2,1,2,1024]{3,2,1,0:T(2,128)} %param.12) | copy-start | bytes 49156

commit v6 on v5

--- a/solution.py
+++ b/solution.py
@@ -247,20 +247,22 @@
 
     def deposit(half):
         filled = fill[core].astype(F32)
+        held = jnp.zeros((1, CHUNK), F32)
         for first in range(0, parts, CHUNK):
             here = pl.ds(half * parts + first, CHUNK)
             rows = cells[half, 0:1, first : first + CHUNK]
             cols = cells[half, 1:2, first : first + CHUNK]
             both = (charge, charge_other)[half][:, first : first + CHUNK].astype(F32)
             weight = jnp.where(core == 0, both[0:1], both[1:2]) * filled
+            held = held + weight
             row_hot[:, here] = jnp.where(cell_iota == rows, 1.0, 0.0).astype(BF16)
             col_hot[:, here] = jnp.where(cell_iota == cols, weight, 0.0).astype(BF16)
         span = pl.ds(half * parts, parts)
-        return mm_nt(row_hot[:, span], col_hot[:, span])
+        return mm_nt(row_hot[:, span], col_hot[:, span]), held
 
     for load in loads[2:]:
         load.wait()
-    density = deposit(0)
+    density, held = deposit(0)
     for swap in swaps:
         swap.wait_recv()
 
@@ -280,14 +282,16 @@
         copy.start()
         packs.append(copy)
 
-    density = density + deposit(1)
+    density_more, held_more = deposit(1)
+    density = density + density_more
+    level = jnp.sum(held + held_more, axis=1, keepdims=True) * (1.0 / (16.0 * GRID))
     basis_high, basis_low = row_basis[0][...], row_basis[1][...]
     pieces = split(density)
     partial = mm3((basis_high[:HALF], basis_low[:HALF]), pieces)
     rows_out[:HALF, :] = partial.astype(BF16)
     top = partial[0:16]
     first_row = lax.broadcasted_iota(jnp.int32, top.shape, 0) == 0
-    rows_out[0:16, :] = jnp.where(first_row, top - jnp.mean(top, axis=1, keepdims=True), top).astype(BF16)
+    rows_out[0:16, :] = jnp.where(first_row, top - level, top).astype(BF16)
     sums = [[] for _ in range(HALVES)]
     for part in range(HALVES):
         if part == 1:

time: 36.4 us -> 36.3 us (level)
  no operation moved by 1% of the time
where the time goes in v6:
time: 36.3 us; the launch traced here: 36 us
  Pallas kernels  34.7 us (96%)
  other arithmetic  1.33 us (4%)
    pallas_call x1, Pallas kernels, body(): pl.pallas_call(functools.partial(kernel, bunches), out_shape=jax.ShapeDty...  34.7 us
    add x1, other arithmetic, body(): return momenta + kicks  1.33 us

profile of v6, /device:TPU:1, one launch (start us, length us, event | category | flops | bytes accessed | tf_op | source)
XLA Modules:
  0.0 36.0 jit_solution(17828678108328435079)
XLA Ops:
  0.0 0.0 copy-start
  0.0 34.7 %shard_map.100 = f32[2,1,2,1024]{3,2,1,0:T(2,128)} custom-call(s32[2,1,2,1024]{3,2,1,0:T(2,128)} %cell_ref.1, bf16[2,1024]{1,0:T(2,128)(2,1)} %bitcast.9, s32[2]{0:T(128)} %bitcast.11, s32[4,4]{1,0:T(4,128)} %bitcast.10, f32[16,256]{1,0:T(8,128)} %bitcast.8, f32[4]{0:T(128)} %stop_ref.1, f32[4]{0:T(128)} %para_ref.1, ...), custom_call_target="tpu_custom_call" | custom-call | tf_op jit(solution)/shard_map/pallas_call | solution.py:520
  34.7 0.0 copy-done
  34.7 1.3 %add.3 = f32[2,1,2,1024]{3,2,1,0:T(2,128)} add(f32[2,1,2,1024]{3,2,1,0:T(2,128)S(1)} %copy-done, f32[2,1,2,1024]{3,2,1,0:T(2,128)} %shard_map.100) | non-fusion elementwise | flops 4096 | bytes 49152 | tf_op jit(solution)/shard_map/add | solution.py:574
Async XLA Ops:
  0.0 34.7 %copy-start = (f32[2,1,2,1024]{3,2,1,0:T(2,128)S(1)}, f32[2,1,2,1024]{3,2,1,0:T(2,128)}, u32[]{:S(2)}) copy-start(f32[2,1,2,1024]{3,2,1,0:T(2,128)} %param.12) | copy-start | bytes 49156

commit v7 on v5

--- a/solution.py
+++ b/solution.py
@@ -24,7 +24,7 @@
 MESH = pl.DeviceIdType.MESH
 F32 = jnp.float32
 BF16 = jnp.bfloat16
-RING_ORDER = (4, 3, 5, 2, 6, 1, 7)
+RING_ORDER = (4, 5, 3, 6, 2, 7, 1)
 
 
 def split_np(table):

time: 36.4 us -> 36.4 us (level)
  no operation moved by 1% of the time
where the time goes in v7:
time: 36.4 us; the launch traced here: 36.1 us
  Pallas kernels  34.7 us (95%)
  other arithmetic  1.33 us (4%)
    pallas_call x1, Pallas kernels, body(): pl.pallas_call(functools.partial(kernel, bunches), out_shape=jax.ShapeDty...  34.7 us
    add x1, other arithmetic, body(): return momenta + kicks  1.33 us

profile of v7, /device:TPU:1, one launch (start us, length us, event | category | flops | bytes accessed | tf_op | source)
XLA Modules:
  0.0 36.1 jit_solution(17087727549977143272)
XLA Ops:
  0.0 0.0 copy-start
  0.0 34.7 %shard_map.100 = f32[2,1,2,1024]{3,2,1,0:T(2,128)} custom-call(s32[2,1,2,1024]{3,2,1,0:T(2,128)} %cell_ref.1, bf16[2,1024]{1,0:T(2,128)(2,1)} %bitcast.9, s32[2]{0:T(128)} %bitcast.11, s32[4,4]{1,0:T(4,128)} %bitcast.10, f32[16,256]{1,0:T(8,128)} %bitcast.8, f32[4]{0:T(128)} %stop_ref.1, f32[4]{0:T(128)} %para_ref.1, ...), custom_call_target="tpu_custom_call" | custom-call | tf_op jit(solution)/shard_map/pallas_call | solution.py:516
  34.7 0.0 copy-done
  34.7 1.3 %add.3 = f32[2,1,2,1024]{3,2,1,0:T(2,128)} add(f32[2,1,2,1024]{3,2,1,0:T(2,128)S(1)} %copy-done, f32[2,1,2,1024]{3,2,1,0:T(2,128)} %shard_map.100) | non-fusion elementwise | flops 4096 | bytes 49152 | tf_op jit(solution)/shard_map/add | solution.py:570
Async XLA Ops:
  0.0 34.7 %copy-start = (f32[2,1,2,1024]{3,2,1,0:T(2,128)S(1)}, f32[2,1,2,1024]{3,2,1,0:T(2,128)}, u32[]{:S(2)}) copy-start(f32[2,1,2,1024]{3,2,1,0:T(2,128)} %param.12) | copy-start | bytes 49156
